TPU v7x, 128 devices: a whole 4x4x4 slice. The times are simulated.
128 devices in a mesh: samp: 32 (over z, y, core), var: 4 (over x).
Axes of the slice: x: 4, y: 4, z: 4, core: 2. Of those that a mesh axis runs over, the one named last changes fastest.
Arguments:
- geno: int32 [65536, 8192], P('samp', 'var'), may hold values from 0 to 2, as said below
- allele_pct: int32 [8192], P('var'), may hold values from 5 to 50
- test_geno: int32 [65536, 2048], P('samp', 'var'), may hold values from 0 to 2, as said below
- test_pct: int32 [2048], P('var'), may hold values from 5 to 50
- exposure: float32 [65536], P('samp'), may hold values from -4 to 4
- perm: int32 [8, 65536], P(None, 'samp'), may hold values from 0 to 65535, each once within a row
- var_comp: float32 [3], replicated, may hold values from 0.3 to 1.5
- solution: float32 [8, 65536], P(None, 'samp'), may hold values from -6 to 6
- resid: float32 [8, 65536], P(None, 'samp'), may hold values from -32 to 32
- direction: float32 [8, 65536], P(None, 'samp'), may hold values from -32 to 32
Outputs:
- new_solution: float32 [8, 65536], P(None, 'samp')
- new_resid: float32 [8, 65536], P(None, 'samp')
- new_direction: float32 [8, 65536], P(None, 'samp')
- assoc_scores: float32 [16, 2048], P(None, 'var')
Inputs may be any that keep to these rules, and one draw needn't show every extreme that they name: `geno`: dosages of a variant follow its allele frequency. `test_geno`: dosages of a variant follow its allele frequency.
All inputs are finite; a program needn't handle non-finite values.
Results may differ from a plain program's by a relative error of at most 0.00016.
Values sent between devices are 32-bit elements; how exact they have to be, the bound alone decides.
A program may use at most 64 MiB of HBM per device.

v0:
```python
import math

import jax
import jax.numpy as jnp
from jax import lax
from jax.sharding import PartitionSpec as P

SLAB = 8192


def standardize(codes, pct):
    freq = pct.astype(jnp.float32) / 100.0
    return (codes.astype(jnp.float32) - 2.0 * freq) * lax.rsqrt(2.0 * freq * (1.0 - freq))


def against_columns(left, right):
    return lax.dot_general(
        left,
        right,
        (((1,), (1,)), ((), ())),
        precision=lax.Precision.HIGHEST,
        preferred_element_type=jnp.float32,
    )


def plain_product(left, right):
    return jnp.dot(left, right, precision=lax.Precision.HIGHEST, preferred_element_type=jnp.float32)


def local(
    geno, allele_pct, test_geno, test_pct, exposure, perm, var_comp, solution, resid, direction
):
    rhs_count = resid.shape[0]
    row_count = resid.shape[1]
    full_exposure = lax.all_gather(exposure, "samp", axis=0, tiled=True)
    shuffled = jnp.take(full_exposure, perm, axis=0)
    loadings = standardize(geno, allele_pct)
    stacked = jnp.concatenate([direction, shuffled * direction], axis=0)
    partial_value = plain_product(stacked, loadings)
    summed = lax.psum(partial_value, "samp")
    applied = against_columns(summed, loadings)
    kernel_rows = lax.psum(applied, "var")
    image = (
        var_comp[0] * direction
        + (var_comp[1] * kernel_rows[:rhs_count] + var_comp[2] * shuffled * kernel_rows[rhs_count:])
        / SLAB
    )
    markers = standardize(test_geno, test_pct)
    norm_now = lax.psum(jnp.sum(resid * resid, axis=1), "samp")
    curvature_sum = lax.psum(jnp.sum(direction * image, axis=1), "samp")
    alpha = norm_now / curvature_sum
    new_resid = resid - alpha[:, None] * image
    norm_next = lax.psum(jnp.sum(new_resid * new_resid, axis=1), "samp")
    new_solution = solution + alpha[:, None] * direction
    new_direction = new_resid + (norm_next / norm_now)[:, None] * direction
    root_count = math.sqrt(row_count * lax.axis_size("samp"))
    stacked_resid = jnp.concatenate([new_resid, shuffled * new_resid], axis=0)
    assoc_scores = lax.psum(plain_product(stacked_resid, markers), "samp") / root_count
    return (new_solution, new_resid, new_direction, assoc_scores)


def solution(mesh):
    return jax.shard_map(
        local,
        mesh=mesh,
        in_specs=(
            P("samp", "var"),
            P("var"),
            P("samp", "var"),
            P("var"),
            P("samp"),
            P(None, "samp"),
            P(),
            P(None, "samp"),
            P(None, "samp"),
            P(None, "samp"),
        ),
        out_specs=(P(None, "samp"), P(None, "samp"), P(None, "samp"), P(None, "var")),
        check_vma=False,
    )
```

profile of v0, /device:TPU:1, one launch (start us, length us, event | category | flops | bytes accessed | tf_op | source)
XLA Modules:
  0.0 499.3 jit_solution(3495116701495570482)
XLA Ops:
  7.2 0.0 all-reduce.5.cloned.1.call-start
  7.2 27.7 %all_gather.3 = f32[65536]{0:T(1024)S(1)} all-gather(f32[2048]{0:T(1024)} %param.14), channel_id=1, replica_groups=mesh['samp'=32,'var'=4] {'samp'}, dimensions={0}, use_global_device_ids=true | all-gather | bytes 270336 | tf_op jit(solution)/shard_map/all_gather | solution.py:35
  34.9 0.8 fusion.21
  35.8 0.0 copy-start.5
  35.8 0.0 copy-start.1
  35.8 0.0 copy-start.2
  35.8 90.5 %gather_fusion = f32[16384]{0:T(1024)S(1)} fusion(f32[65536]{0:T(1024)S(1)} %all_gather.3, s32[16384]{0:T(1024)S(1)} %broadcast_clamp_fusion), kind=kCustom, calls=%fused_computation | custom fusion | bytes 196608 | tf_op jit(solution)/shard_map/jit(_take)/gather | solution.py:36
  126.4 0.0 copy-start.7
  126.4 0.0 copy-done.5
  126.5 0.0 copy-start.6
  126.5 0.0 copy-start.3
  126.5 0.0 copy-start.4
  126.5 13.6 %fusion.1 = f32[16,2048]{1,0:T(8,128)} fusion(s32[2048,2048]{1,0:T(8,128)} %param.10, f32[2048]{0:T(1024)S(1)} %get-tuple-element.15, f32[2048]{0:T(1024)S(1)} %get-tuple-element.14, f32[8,2048]{1,0:T(8,128)S(1)} %fusion.25, f32[8,2048]{1,0:T(8,128)S(1)} %copy-done.1), kind=kOutput, calls=%fused_computation.3 | convolution fusion | flops 817922048 | bytes 17055744 | tf_op jit(solution)/shard_map/dot_general | solution.py:27
  140.1 0.0 all-reduce.5.cloned.1.call-update
  140.2 0.2 all-reduce.7.cloned.1.call-start
  140.4 0.0 copy-done.7
  140.4 100.0 %all-reduce.5.cloned.1.call-done = f32[16,2048]{1,0:T(8,128)} async-done(((f32[16,2048]{1,0:T(8,128)}), f32[16,2048]{1,0:T(8,128)}) %all-reduce.5.cloned.1.call-update) | async-done | bytes 131088 | tf_op jit(solution)/shard_map/psum | solution.py:40
  240.4 18.1 %fusion = f32[16,2048]{1,0:T(8,128)} fusion(f32[16,2048]{1,0:T(8,128)} %all-reduce.5.cloned.1.call-done, s32[2048,2048]{1,0:T(8,128)} %param.10, f32[2048]{0:T(1024)S(1)} %get-tuple-element.15, f32[2048]{0:T(1024)S(1)} %get-tuple-element.14), kind=kOutput, calls=%fused_computation.2 | convolution fusion | flops 817889280 | bytes 17055744 | tf_op jit(solution)/shard_map/dot_general | solution.py:17
  258.5 0.0 all-reduce.7.cloned.1.call-update
  258.5 0.0 copy-done.6
  258.5 0.6 fusion.27
  259.1 0.1 multiply_reduce_fusion.2
  259.2 38.0 %all-reduce.7.cloned.1.call-done = f32[16,2048]{1,0:T(8,128)} async-done(((f32[16,2048]{1,0:T(8,128)}), f32[16,2048]{1,0:T(8,128)}) %all-reduce.7.cloned.1.call-update) | async-done | bytes 131088 | tf_op jit(solution)/shard_map/psum | solution.py:42
  297.2 3.0 multiply_reduce_fusion.1
  300.2 64.9 %all-reduce.1 = (f32[8]{0:T(128)S(1)}, f32[8]{0:T(128)S(1)}) all-reduce(f32[8]{0:T(128)S(1)} %multiply_reduce_fusion.2, f32[8]{0:T(128)S(1)} %get-tuple-element.10), channel_id=1, replica_groups=mesh['samp'=32,'var'=4] {'samp'}, use_global_device_ids=true, to_apply=%region_1.2 | all-reduce | flops 16 | bytes 128 | tf_op jit(solution)/shard_map/psum | solution.py:49
  365.1 0.1 fusion.24
  365.2 0.0 copy-start
  365.3 4.7 fusion.6
  369.9 0.1 multiply_reduce_fusion
  370.1 121.1 %all-reduce = (f32[8]{0:T(128)S(1)}, f32[16,512]{1,0:T(8,128)S(1)}) all-reduce(f32[8]{0:T(128)S(1)} %multiply_reduce_fusion, f32[16,512]{1,0:T(8,128)S(1)} %fusion.6), channel_id=1, replica_groups=mesh['samp'=32,'var'=4] {'samp'}, use_global_device_ids=true, to_apply=%region_7.8 | all-reduce | flops 8200 | bytes 65600 | tf_op jit(solution)/shard_map/psum | solution.py:53
  491.2 0.6 broadcast_multiply_fusion
  491.8 0.7 multiply_add_fusion
  (13 shorter events, 0.1 us)
Async XLA Ops:
  7.2 233.2 %all-reduce.5.cloned.1.call-start = ((), (), s32[]{:S(2)}) async-start(), calls=%async_computation | async-start | bytes 262144 | tf_op jit(solution)/shard_map/psum | solution.py:40
  35.8 90.6 %copy-start.5 = (s32[2048]{0:T(1024)S(1)}, s32[2048]{0:T(1024)}, u32[]{:S(2)}) copy-start(s32[2048]{0:T(1024)} %param.11) | copy-start | bytes 24580
  35.8 90.6 %copy-start.1 = (f32[8,2048]{1,0:T(8,128)S(1)}, f32[8,2048]{1,0:T(8,128)}, u32[]{:S(2)}) copy-start(f32[8,2048]{1,0:T(8,128)} %param.19) | copy-start | bytes 196612
  35.8 90.6 %copy-start.2 = (s32[8,2048]{1,0:T(8,128)S(1)}, s32[8,2048]{1,0:T(8,128)}, u32[]{:S(2)}) copy-start(s32[8,2048]{1,0:T(8,128)} %param.15) | copy-start | bytes 196612
  126.4 14.0 %copy-start.7 = (s32[512]{0:T(512)S(1)}, s32[512]{0:T(512)}, u32[]{:S(2)}) copy-start(s32[512]{0:T(512)} %param.13) | copy-start | bytes 6148
  126.5 132.0 %copy-start.6 = (f32[3]{0:T(128)S(1)}, f32[3]{0:T(128)}, u32[]{:S(2)}) copy-start(f32[3]{0:T(128)} %param.16) | copy-start | bytes 40
  126.5 132.6 %copy-start.3 = (f32[8,2048]{1,0:T(8,128)S(1)}, f32[8,2048]{1,0:T(8,128)}, u32[]{:S(2)}) copy-start(f32[8,2048]{1,0:T(8,128)} %param.18) | copy-start | bytes 196612
  126.5 365.3 %copy-start.4 = (f32[8,2048]{1,0:T(8,128)S(1)}, f32[8,2048]{1,0:T(8,128)}, u32[]{:S(2)}) copy-start(f32[8,2048]{1,0:T(8,128)} %param.17) | copy-start | bytes 196612
  140.2 157.1 %all-reduce.7.cloned.1.call-start = ((), (), s32[]{:S(2)}) async-start(), calls=%async_computation.1 | async-start | bytes 262144 | tf_op jit(solution)/shard_map/psum | solution.py:42
  365.2 127.3 %copy-start = (f32[8,2048]{1,0:T(8,128)}, f32[8,2048]{1,0:T(8,128)S(1)}, u32[]{:S(2)}) copy-start(f32[8,2048]{1,0:T(8,128)S(1)} %get-tuple-element.9) | copy-start | bytes 196612
Sparse Core Ops, SparseCore 0:
  140.3 100.0 all-reduce.4
  258.6 38.5 all-reduce.6
where the time goes:
time: 504 us; the launch traced here: 499 us
  blocking collectives  214 us (42%)
  waiting for transfers between devices  138 us (27%)
  local copies, waits for them, and re-layouts  91.2 us (18%)
  matrix products  36.4 us (7%)
  between operations  14.2 us (3%)
  other arithmetic  5.56 us (1%)
    psum x1, blocking collectives, local(): norm_next = lax.psum(jnp.sum(new_resid * new_resid, axis=1), 'samp')  121 us
    psum x1, waiting for transfers between devices, local(): summed = lax.psum(partial_value, 'samp')  100 us
    gather x2, local copies, waits for them, and re-layouts, local(): shuffled = jnp.take(full_exposure, perm, axis=0)  90.6 us
    psum x1, blocking collectives, local(): norm_now = lax.psum(jnp.sum(resid * resid, axis=1), 'samp')  64.9 us
    psum x1, waiting for transfers between devices, local(): kernel_rows = lax.psum(applied, 'var')  38 us
    all_gather x1, blocking collectives, local(): full_exposure = lax.all_gather(exposure, 'samp', axis=0, tiled=True)  27.7 us
    dot_general x2, matrix products, plain_product(): jnp.dot(left, right, precision=lax.Precision.HIGHEST, preferred_element_t...  18.3 us
    dot_general x1, matrix products, against_columns(): lax.dot_general(left, right, (((1,), (1,)), ((), ())), precision=lax.Prec...  18.1 us
  transfers between devices with their start and end apart: 2, of which 2 were waited for; matrix products, arithmetic and copies ran while one was open for 0% of the time, Pallas kernels for 0%

commit v1 on v0

v1 whole, which is shorter than its diff:
```python
import functools

import jax
import jax.numpy as jnp
from jax import lax
from jax.experimental import pallas as pl
from jax.experimental.pallas import tpu as pltpu
from jax.sharding import PartitionSpec as P

MESH = pl.DeviceIdType.MESH
F32 = jnp.float32
BF16 = jnp.bfloat16


def log2(n):
    return n.bit_length() - 1


def split3(value):
    high = value.astype(BF16)
    rest = value - high.astype(F32)
    mid = rest.astype(BF16)
    low = (rest - mid.astype(F32)).astype(BF16)
    return high, mid, low


def sum3(value):
    rows = value.shape[0] // 3
    return value[:rows] + value[rows : 2 * rows] + value[2 * rows :]


def kernel(
    dims,
    geno_hbm, tgeno_hbm, pct_ref, tpct_ref, expo_ref, perm_ref, vc_ref, sol_ref, res_ref, dir_ref,
    osol_ref, ores_ref, odir_ref, oassoc_ref,
    graw, traw, gbf, tbf, table, tparts, shuf, parts, apart,
    psend, precv, pz, pall, qsend, qrecv, imgs, fsend, frecv, fz, fall,
    gsem, tsem, sem_ez, sem_ej, sem_sh, sem_p, sem_pz, sem_pa, sem_q, sem_im, sem_f, sem_fz, sem_fa,
):
    NZ, NJ, NX, scale_rows = dims
    samp = lax.axis_index("samp")
    x = lax.axis_index("var")
    z = samp // NJ
    j = samp % NJ
    SP = dir_ref.shape[1]
    V = pct_ref.shape[1]
    TV = tpct_ref.shape[1]
    RP = SP // 128
    VB = V // NJ
    SQ = SP // NX
    chunks = graw.shape[0]
    crows = graw.shape[1]
    tchunks = traw.shape[0]
    trows = traw.shape[1]

    for i in range(chunks):
        pltpu.make_async_copy(geno_hbm.at[pl.ds(i * crows, crows), :], graw.at[i], gsem.at[i]).start()
    for i in range(tchunks):
        pltpu.make_async_copy(tgeno_hbm.at[pl.ds(i * trows, trows), :], traw.at[i], tsem.at[i]).start()

    def to_j(peer):
        return {"samp": z * NJ + peer}

    def to_z(peer):
        return {"samp": peer * NJ + j}

    def to_x(peer):
        return {"var": peer}

    groups = {"j": (j, NJ, to_j), "z": (z, NZ, to_z), "x": (x, NX, to_x)}

    def each_peer(group, body):
        me, count, _ = groups[group]

        def step(off, carry):
            body((me + off) % count)
            return carry

        lax.fori_loop(1, count, step, 0)

    def push(group, src, dst, sem, peer):
        me, _, place = groups[group]
        pltpu.make_async_remote_copy(
            src_ref=src, dst_ref=dst, send_sem=sem.at[0, peer], recv_sem=sem.at[1, me],
            device_id=place(peer), device_id_type=MESH,
        ).start()

    def arrived(group, dst_of, sem):
        me, _, place = groups[group]

        def one(peer):
            pltpu.make_async_remote_copy(
                src_ref=dst_of(peer), dst_ref=dst_of(peer), send_sem=sem.at[0, peer], recv_sem=sem.at[1, peer],
                device_id=place(peer), device_id_type=MESH,
            ).wait_recv()

        each_peer(group, one)

    def sent(group, src_of, sem):
        _, _, place = groups[group]

        def one(peer):
            pltpu.make_async_remote_copy(
                src_ref=src_of(peer), dst_ref=src_of(peer), send_sem=sem.at[0, peer], recv_sem=sem.at[1, peer],
                device_id=place(peer), device_id_type=MESH,
            ).wait_send()

        each_peer(group, one)

    barrier = pltpu.get_barrier_semaphore()
    for group in ("j", "z", "x"):
        place = groups[group][2]
        each_peer(group, lambda peer, place=place: pl.semaphore_signal(barrier, inc=1, device_id=place(peer), device_id_type=MESH))
    pl.semaphore_wait(barrier, NJ + NZ + NX - 3)

    each_peer("z", lambda peer: push("z", expo_ref, table.at[j, z], sem_ez, peer))
    table[j, z] = expo_ref[...]

    pct = pct_ref[...].astype(F32)
    tpct = tpct_ref[...].astype(F32)

    def convert(i):
        pltpu.make_async_copy(geno_hbm.at[pl.ds(i * crows, crows), :], graw.at[i], gsem.at[i]).wait()
        block = 32

        def rows(r, carry):
            start = pl.multiple_of(r * block, block)
            codes = graw[i, pl.ds(start, block), :].astype(F32)
            gbf[pl.ds(pl.multiple_of(i * crows + start, block), block), :] = (codes * 50.0 - pct).astype(BF16)
            return carry

        lax.fori_loop(0, crows // block, rows, 0)

    def tconvert(i):
        pltpu.make_async_copy(tgeno_hbm.at[pl.ds(i * trows, trows), :], traw.at[i], tsem.at[i]).wait()
        block = 64

        def rows(r, carry):
            start = pl.multiple_of(r * block, block)
            codes = traw[i, pl.ds(start, block), :].astype(F32)
            tbf[pl.ds(pl.multiple_of(i * trows + start, block), block), :] = (codes * 50.0 - tpct).astype(BF16)
            return carry

        lax.fori_loop(0, trows // block, rows, 0)

    half = chunks // 2

    def convert_step(i, carry):
        convert(i)
        return carry

    def tconvert_step(i, carry):
        tconvert(i)
        return carry

    lax.fori_loop(0, half, convert_step, 0)

    arrived("z", lambda peer: table.at[j, peer], sem_ez)
    each_peer("j", lambda peer: push("j", table.at[j], table.at[j], sem_ej, peer))

    lax.fori_loop(half, chunks, convert_step, 0)
    lax.fori_loop(0, tchunks, tconvert_step, 0)

    arrived("j", lambda peer: table.at[peer], sem_ej)

    rows_all = NJ * NZ * RP
    flat = table[...].reshape(rows_all, 128)
    high, mid, low = split3(flat.T)
    tparts[0:128, :] = high
    tparts[128:256, :] = mid
    tparts[256:384, :] = low
    index = perm_ref[:, pl.ds(pl.multiple_of(x * SQ, SQ), SQ)]
    row_z = index >> log2(SP * NJ)
    row_j = (index >> log2(SP)) & (NJ - 1)
    row_r = (index >> 7) & (RP - 1)
    row_of = (row_j * NZ + row_z) * RP + row_r
    lane_of = index & 127
    width = min(SQ, 256)
    for b in range(8):
        for c in range(SQ // width):
            cols = slice(c * width, (c + 1) * width)
            hit = lax.broadcasted_iota(jnp.int32, (rows_all, width), 0) == row_of[b : b + 1, cols]
            onehot = jnp.where(hit, 1.0, 0.0).astype(BF16)
            picked = sum3(jnp.dot(tparts[...], onehot, preferred_element_type=F32))
            lane_hit = lax.broadcasted_iota(jnp.int32, (128, width), 0) == lane_of[b : b + 1, cols]
            shuf[x, b : b + 1, cols] = jnp.sum(jnp.where(lane_hit, picked, 0.0), axis=0, keepdims=True)
    each_peer("x", lambda peer: push("x", shuf.at[x], shuf.at[x], sem_sh, peer))
    arrived("x", lambda peer: shuf.at[peer], sem_sh)

    def fill(value_of):
        for q in range(NX):
            value = value_of(q)
            stacked = jnp.concatenate([value, shuf[q] * value], axis=0)
            high, mid, low = split3(stacked)
            cols = slice(q * SQ, (q + 1) * SQ)
            parts[0:16, cols] = high
            parts[16:32, cols] = mid
            parts[32:48, cols] = low

    fill(lambda q: dir_ref[:, q * SQ : (q + 1) * SQ])

    def product(block):
        cols = pl.ds(pl.multiple_of(block * VB, VB), VB)
        return sum3(jnp.dot(parts[...], gbf[:, cols], preferred_element_type=F32))

    def product_step(peer):
        psend[peer] = product(peer)
        push("j", psend.at[peer], precv.at[j], sem_p, peer)

    each_peer("j", product_step)
    precv[j] = product(j)

    fill(lambda q: res_ref[:, q * SQ : (q + 1) * SQ])
    apart[...] = sum3(jnp.dot(parts[...], tbf[...], preferred_element_type=F32))

    arrived("j", lambda peer: precv.at[peer], sem_p)
    total = precv[0]
    for i in range(1, NJ):
        total = total + precv[i]
    pz[z] = total
    each_peer("z", lambda peer: push("z", pz.at[z], pz.at[z], sem_pz, peer))
    arrived("z", lambda peer: pz.at[peer], sem_pz)
    total = pz[0]
    for i in range(1, NZ):
        total = total + pz[i]
    pall[j] = total
    each_peer("j", lambda peer: push("j", pall.at[j], pall.at[j], sem_pa, peer))
    freq = pct / 100.0
    square = 1.0 / (2.0 * freq * (1.0 - freq)) / 2500.0
    arrived("j", lambda peer: pall.at[peer], sem_pa)

    for i in range(NJ):
        cols = slice(i * VB, (i + 1) * VB)
        high, mid, low = split3(pall[i] * square[:, cols])
        parts[0:16, cols] = high
        parts[16:32, cols] = mid
        parts[32:48, cols] = low

    def back(part):
        rows = pl.ds(pl.multiple_of(part * SQ, SQ), SQ)
        return sum3(
            lax.dot_general(parts[...], gbf[rows, :], (((1,), (1,)), ((), ())), preferred_element_type=F32)
        )

    def back_step(peer):
        qsend[peer] = back(peer)
        push("x", qsend.at[peer], qrecv.at[x], sem_q, peer)

    each_peer("x", back_step)
    qrecv[x] = back(x)
    arrived("x", lambda peer: qrecv.at[peer], sem_q)
    rows_sum = qrecv[0]
    for i in range(1, NX):
        rows_sum = rows_sum + qrecv[i]
    own_dir = dir_ref[:, pl.ds(pl.multiple_of(x * SQ, SQ), SQ)]
    imgs[x] = vc_ref[0] * own_dir + (vc_ref[1] * rows_sum[0:8] + vc_ref[2] * shuf[x] * rows_sum[8:16]) * (1.0 / scale_rows)
    each_peer("x", lambda peer: push("x", imgs.at[x], imgs.at[x], sem_im, peer))
    arrived("x", lambda peer: imgs.at[peer], sem_im)

    fill(lambda q: imgs[q])
    bpart = sum3(jnp.dot(parts[...], tbf[...], preferred_element_type=F32))
    sums = [jnp.zeros((8, 1), F32) for _ in range(4)]
    for q in range(NX):
        cols = slice(q * SQ, (q + 1) * SQ)
        d, r, im = dir_ref[:, cols], res_ref[:, cols], imgs[q]
        for k, term in enumerate((r * r, d * im, r * im, im * im)):
            sums[k] = sums[k] + jnp.sum(term, axis=1, keepdims=True)
    lane = lax.broadcasted_iota(jnp.int32, (8, 128), 1)
    scalars = jnp.where(lane == 0, sums[0], jnp.where(lane == 1, sums[1], jnp.where(lane == 2, sums[2], sums[3])))
    quarters = TV // 128
    for i in range(NJ):
        h, q = divmod(i, quarters)
        fsend[i, 0] = apart[8 * h : 8 * h + 8, 128 * q : 128 * q + 128]
        fsend[i, 1] = bpart[8 * h : 8 * h + 8, 128 * q : 128 * q + 128]
        fsend[i, 2] = scalars
    each_peer("j", lambda peer: push("j", fsend.at[peer], frecv.at[j], sem_f, peer))
    frecv[j] = fsend[j]
    arrived("j", lambda peer: frecv.at[peer], sem_f)
    total = frecv[0]
    for i in range(1, NJ):
        total = total + frecv[i]
    fz[z] = total
    each_peer("z", lambda peer: push("z", fz.at[z], fz.at[z], sem_fz, peer))
    arrived("z", lambda peer: fz.at[peer], sem_fz)
    total = fz[0]
    for i in range(1, NZ):
        total = total + fz[i]
    norm_now = total[2][:, 0:1]
    curvature = total[2][:, 1:2]
    alpha = norm_now / curvature
    fall[j] = total[0] - alpha * total[1]
    each_peer("j", lambda peer: push("j", fall.at[j], fall.at[j], sem_fa, peer))

    norm_next = norm_now - 2.0 * alpha * total[2][:, 2:3] + alpha * alpha * total[2][:, 3:4]
    beta = norm_next / norm_now
    for q in range(NX):
        cols = slice(q * SQ, (q + 1) * SQ)
        d = dir_ref[:, cols]
        new_res = res_ref[:, cols] - alpha * imgs[q]
        osol_ref[:, cols] = sol_ref[:, cols] + alpha * d
        ores_ref[:, cols] = new_res
        odir_ref[:, cols] = new_res + beta * d

    tfreq = tpct / 100.0
    root = (scale_rows_root(dims, SP)) * 50.0
    tscale = lax.rsqrt(2.0 * tfreq * (1.0 - tfreq)) / root
    arrived("j", lambda peer: fall.at[peer], sem_fa)
    for i in range(NJ):
        h, q = divmod(i, quarters)
        cols = slice(128 * q, 128 * q + 128)
        oassoc_ref[8 * h : 8 * h + 8, cols] = fall[i] * tscale[:, cols]

    sent("z", lambda peer: expo_ref, sem_ez)
    sent("j", lambda peer: table.at[j], sem_ej)
    sent("x", lambda peer: shuf.at[x], sem_sh)
    sent("j", lambda peer: psend.at[peer], sem_p)
    sent("z", lambda peer: pz.at[z], sem_pz)
    sent("j", lambda peer: pall.at[j], sem_pa)
    sent("x", lambda peer: qsend.at[peer], sem_q)
    sent("x", lambda peer: imgs.at[x], sem_im)
    sent("j", lambda peer: fsend.at[peer], sem_f)
    sent("z", lambda peer: fz.at[z], sem_fz)
    sent("j", lambda peer: fall.at[j], sem_fa)


def scale_rows_root(dims, per_device):
    return float(dims[0] * dims[1] * per_device) ** 0.5


def local(dims, geno, allele_pct, test_geno, test_pct, exposure, perm, var_comp, solution, resid, direction):
    NZ, NJ, NX, _ = dims
    SP, V = geno.shape
    TV = test_geno.shape[1]
    RP, VB, SQ = SP // 128, V // NJ, SP // NX
    chunks, tchunks = 8, 2
    vmem = pl.BlockSpec(memory_space=pltpu.VMEM)
    hbm = pl.BlockSpec(memory_space=pl.ANY)
    smem = pl.BlockSpec(memory_space=pltpu.SMEM)
    dma = pltpu.SemaphoreType.DMA
    rhs = jax.ShapeDtypeStruct((8, SP), F32)
    return pl.pallas_call(
        functools.partial(kernel, dims),
        out_shape=(rhs, rhs, rhs, jax.ShapeDtypeStruct((16, TV), F32)),
        in_specs=[hbm, hbm, vmem, vmem, vmem, vmem, smem, vmem, vmem, vmem],
        out_specs=(vmem, vmem, vmem, vmem),
        scratch_shapes=[
            pltpu.VMEM((chunks, SP // chunks, V), jnp.int32),
            pltpu.VMEM((tchunks, SP // tchunks, TV), jnp.int32),
            pltpu.VMEM((SP, V), BF16),
            pltpu.VMEM((SP, TV), BF16),
            pltpu.VMEM((NJ, NZ, RP, 128), F32),
            pltpu.VMEM((384, NJ * NZ * RP), BF16),
            pltpu.VMEM((NX, 8, SQ), F32),
            pltpu.VMEM((48, max(SP, V)), BF16),
            pltpu.VMEM((16, TV), F32),
            pltpu.VMEM((NJ, 16, VB), F32),
            pltpu.VMEM((NJ, 16, VB), F32),
            pltpu.VMEM((NZ, 16, VB), F32),
            pltpu.VMEM((NJ, 16, VB), F32),
            pltpu.VMEM((NX, 16, SQ), F32),
            pltpu.VMEM((NX, 16, SQ), F32),
            pltpu.VMEM((NX, 8, SQ), F32),
            pltpu.VMEM((NJ, 3, 8, 128), F32),
            pltpu.VMEM((NJ, 3, 8, 128), F32),
            pltpu.VMEM((NZ, 3, 8, 128), F32),
            pltpu.VMEM((NJ, 8, 128), F32),
            dma((chunks,)),
            dma((tchunks,)),
            dma((2, NZ)),
            dma((2, NJ)),
            dma((2, NX)),
            dma((2, NJ)),
            dma((2, NZ)),
            dma((2, NJ)),
            dma((2, NX)),
            dma((2, NX)),
            dma((2, NJ)),
            dma((2, NZ)),
            dma((2, NJ)),
        ],
        compiler_params=pltpu.CompilerParams(
            collective_id=0, has_side_effects=True, vmem_limit_bytes=60 * 1024 * 1024
        ),
    )(
        geno,
        test_geno,
        allele_pct.reshape(1, V),
        test_pct.reshape(1, TV),
        exposure.reshape(RP, 128),
        perm,
        var_comp,
        solution,
        resid,
        direction,
    )


def solution(mesh):
    samp, var = mesh.shape["samp"], mesh.shape["var"]
    near = 8 if samp == 32 else samp // 2

    def whole(geno, *rest):
        dims = (samp // near, near, var, float(geno.shape[1]))
        return jax.shard_map(
            functools.partial(local, dims),
            mesh=mesh,
            in_specs=(
                P("samp", "var"),
                P("var"),
                P("samp", "var"),
                P("var"),
                P("samp"),
                P(None, "samp"),
                P(),
                P(None, "samp"),
                P(None, "samp"),
                P(None, "samp"),
            ),
            out_specs=(P(None, "samp"), P(None, "samp"), P(None, "samp"), P(None, "var")),
            check_vma=False,
        )(geno, *rest)

    return whole
```

time: 504 us -> 64.8 us (0.13)
  blocking collectives: 214 us -> 0 us
  waiting for transfers between devices: 138 us -> 0 us
  local copies, waits for them, and re-layouts: 91.2 us -> 5.79 us
  Pallas kernels: 0 us -> 58 us
  matrix products: 36.4 us -> 0 us
  between operations: 14.2 us -> 0.64 us
  other arithmetic: 5.56 us -> 0 us
    psum x2 -> x0, blocking collectives: 186 us -> none  [the longest x1 121 us: local(): norm_next = lax.psum(jnp.sum(new_resid * new_resid, axis=1), 'samp')]
    psum x2 -> x0, waiting for transfers between devices: 138 us -> none  [the longest x1 100 us: local(): summed = lax.psum(partial_value, 'samp')]
    gather x2 -> x0, local copies, waits for them, and re-layouts: 90.6 us -> none  [local(): shuffled = jnp.take(full_exposure, perm, axis=0)]
    pallas_call x0 -> x1, Pallas kernels: none -> 58 us  [local(): pl.pallas_call(functools.partial(kernel, dims), out_shape=(rhs, rhs, rhs,...]
    dot_general x3 -> x0, matrix products: 36.4 us -> none  [the longest x2 18.3 us: plain_product(): jnp.dot(left, right, precision=lax.Precision.HIGHEST, preferred_element_t...]
    all_gather x1 -> x0, blocking collectives: 27.7 us -> none  [local(): full_exposure = lax.all_gather(exposure, 'samp', axis=0, tiled=True)]
    unnamed x17 -> x4, local copies, waits for them, and re-layouts: 0.06 us -> 5.79 us
  transfers between devices with their start and end apart: 2 -> 0, of which waited for: 2 -> 0; matrix products, arithmetic and copies ran while one was open for 0% -> 0% of each run, Pallas kernels for 0% -> 0%
where the time goes in v1:
time: 64.8 us; the launch traced here: 64.5 us
  Pallas kernels  58 us (90%)
  local copies, waits for them, and re-layouts  5.79 us (9%)
    pallas_call x1, Pallas kernels, local(): pl.pallas_call(functools.partial(kernel, dims), out_shape=(rhs, rhs, rhs,...  58 us
    unnamed x4, local copies, waits for them, and re-layouts  5.79 us

profile of v1, /device:TPU:1, one launch (start us, length us, event | category | flops | bytes accessed | tf_op | source)
XLA Modules:
  0.0 64.5 jit_solution(17091372312012843107)
XLA Ops:
  0.6 58.0 %shard_map.129 = (f32[8,2048]{1,0:T(8,128)}, f32[8,2048]{1,0:T(8,128)}, f32[8,2048]{1,0:T(8,128)}, f32[16,512]{1,0:T(8,128)}) custom-call(s32[2048,2048]{1,0:T(8,128)} %geno_hbm.1, s32[2048,512]{1,0:T(8,128)} %tgeno_hbm.1, s32[1,2048]{1,0:T(1,128)} %bitcast.3, s32[1,512]{1,0:T(1,128)} %bitcast.5, f32[16,128]{1,0:T(8,128)} %bitcast.4, s32[8,2048]{1,0:T(8,128)} %perm_ref.1, ...), custom_call_target="tpu_custom_call" | custom-call | tf_op jit(solution)/shard_map/pallas_call | solution.py:341
  58.7 1.5 %copy.18 = f32[8,2048]{1,0:T(8,128)} copy(f32[8,2048]{1,0:T(8,128)} %get-tuple-element.8) | data formatting | bytes 131072
  60.1 1.5 %copy.19 = f32[8,2048]{1,0:T(8,128)} copy(f32[8,2048]{1,0:T(8,128)} %get-tuple-element.9) | data formatting | bytes 131072
  61.6 1.5 %copy.20 = f32[8,2048]{1,0:T(8,128)} copy(f32[8,2048]{1,0:T(8,128)} %get-tuple-element.10) | data formatting | bytes 131072
  63.1 1.4 %copy.21 = f32[16,512]{1,0:T(8,128)} copy(f32[16,512]{1,0:T(8,128)} %get-tuple-element.11) | data formatting | bytes 65536

commit v2 on v1

v2 whole, which is shorter than its diff:
```python
import functools

import jax
import jax.numpy as jnp
from jax import lax
from jax.experimental import pallas as pl
from jax.experimental.pallas import tpu as pltpu
from jax.sharding import PartitionSpec as P

MESH = pl.DeviceIdType.MESH
F32 = jnp.float32
BF16 = jnp.bfloat16


def log2(n):
    return n.bit_length() - 1


def split3(value):
    high = value.astype(BF16)
    rest = value - high.astype(F32)
    mid = rest.astype(BF16)
    low = (rest - mid.astype(F32)).astype(BF16)
    return high, mid, low


def sum3(value):
    rows = value.shape[0] // 3
    return value[:rows] + value[rows : 2 * rows] + value[2 * rows :]


def kernel(
    dims,
    geno_hbm, tgeno_hbm, pct_hbm, tpct_hbm, expo_hbm, perm_hbm, vc_hbm, sol_hbm, res_hbm, dir_hbm,
    osol_ref, ores_ref, odir_ref, oassoc_ref,
    vc_ref, expo_ref, perm_ref, pct_ref, tpct_ref, sol_ref, res_ref, dir_ref,
    graw, traw, gbf, tbf, table, tparts, shuf, parts, lefts, squares, acc,
    psend, precv, pz, pall, asend, arecv, irecv, isend, fsend, frecv, fz, fall,
    isem, gsem, tsem, sem_ez, sem_ej, sem_sh, sem_p, sem_pz, sem_pa, sem_a, sem_im, sem_f, sem_fz, sem_fa,
):
    NZ, NJ, NX, scale_rows = dims
    samp = lax.axis_index("samp")
    x = lax.axis_index("var")
    z = samp // NJ
    j = samp % NJ
    core = j % 2
    pair = j - core
    SP = dir_ref.shape[1]
    V = pct_ref.shape[1]
    TV = tpct_ref.shape[1]
    RP = SP // 128
    VB = V // NJ
    SQ = SP // NX
    W = min(SQ, 256)
    chunks = graw.shape[0]
    crows = graw.shape[1]
    tchunks = traw.shape[0]
    trows = traw.shape[1]

    reads = [
        pltpu.make_async_copy(src, dst, isem.at[i])
        for i, (src, dst) in enumerate((
            (expo_hbm, expo_ref), (pct_hbm, pct_ref), (perm_hbm, perm_ref), (dir_hbm, dir_ref),
            (res_hbm, res_ref), (tpct_hbm, tpct_ref), (sol_hbm, sol_ref), (vc_hbm, vc_ref),
        ))
    ]
    reads[0].start()

    def gread(i):
        return pltpu.make_async_copy(geno_hbm.at[pl.ds(i * crows, crows), :], graw.at[i], gsem.at[i])

    def tread(i):
        return pltpu.make_async_copy(tgeno_hbm.at[pl.ds(i * trows, trows), :], traw.at[i], tsem.at[i])

    def to_j(peer):
        return {"samp": z * NJ + peer}

    def to_z(peer):
        return {"samp": peer * NJ + j}

    def to_x(peer):
        return {"var": peer}

    groups = {"j": (j, NJ, to_j), "z": (z, NZ, to_z), "x": (x, NX, to_x)}

    def each_peer(group, body):
        me, count, _ = groups[group]

        def step(t, carry):
            off = count // 2 + ((t + 1) // 2) * (2 * (t % 2) - 1)
            body((me + off) % count)
            return carry

        lax.fori_loop(0, count - 1, step, 0)

    def push(group, src, dst, sem, peer):
        me, _, place = groups[group]
        pltpu.make_async_remote_copy(
            src_ref=src, dst_ref=dst, send_sem=sem.at[0, peer], recv_sem=sem.at[1, me],
            device_id=place(peer), device_id_type=MESH,
        ).start()

    def arrived_one(group, dst, sem, peer):
        place = groups[group][2]
        pltpu.make_async_remote_copy(
            src_ref=dst, dst_ref=dst, send_sem=sem.at[0, peer], recv_sem=sem.at[1, peer],
            device_id=place(peer), device_id_type=MESH,
        ).wait_recv()

    def arrived(group, dst_of, sem):
        each_peer(group, lambda peer: arrived_one(group, dst_of(peer), sem, peer))

    def sent(group, src_of, sem):
        place = groups[group][2]

        def one(peer):
            pltpu.make_async_remote_copy(
                src_ref=src_of(peer), dst_ref=src_of(peer), send_sem=sem.at[0, peer], recv_sem=sem.at[1, peer],
                device_id=place(peer), device_id_type=MESH,
            ).wait_send()

        each_peer(group, one)

    barrier = pltpu.get_barrier_semaphore()
    for group in ("j", "z", "x"):
        place = groups[group][2]
        each_peer(
            group,
            lambda peer, place=place: pl.semaphore_signal(barrier, inc=1, device_id=place(peer), device_id_type=MESH),
        )
    for copy in reads[1:]:
        copy.start()
    for i in range(chunks):
        gread(i).start()
    for i in range(tchunks):
        tread(i).start()
    reads[0].wait()
    pl.semaphore_wait(barrier, NJ + NZ + NX - 3)

    each_peer("z", lambda peer: push("z", expo_ref, table.at[core, z], sem_ez, peer))
    table[core, z] = expo_ref[...]

    reads[1].wait()
    reads[5].wait()
    pct = pct_ref[...].astype(F32)
    tpct = tpct_ref[...].astype(F32)

    def convert(i, carry):
        gread(i).wait()
        block = 32

        def rows(r, carry):
            start = pl.multiple_of(r * block, block)
            codes = graw[i, pl.ds(start, block), :].astype(F32)
            gbf[pl.ds(pl.multiple_of(i * crows + start, block), block), :] = (codes * 50.0 - pct).astype(BF16)
            return carry

        return lax.fori_loop(0, crows // block, rows, carry)

    def tconvert(i, carry):
        tread(i).wait()
        block = 64

        def rows(r, carry):
            start = pl.multiple_of(r * block, block)
            codes = traw[i, pl.ds(start, block), :].astype(F32)
            tbf[pl.ds(pl.multiple_of(i * trows + start, block), block), :] = (codes * 50.0 - tpct).astype(BF16)
            return carry

        return lax.fori_loop(0, trows // block, rows, carry)

    half = 3 * chunks // 8
    lax.fori_loop(0, half, convert, 0)

    arrived("z", lambda peer: table.at[core, peer], sem_ez)
    each_peer("j", lambda peer: push("j", table.at[core], table.at[(j - (peer - peer % 2) + NJ) % NJ], sem_ej, peer))

    lax.fori_loop(half, chunks, convert, 0)
    freq = pct / 100.0
    square = 1.0 / (2.0 * freq * (1.0 - freq)) / 2500.0
    for i in range(NJ):
        squares[i] = square[:, i * VB : (i + 1) * VB]
    for i in (2, 3, 4, 6, 7):
        reads[i].wait()

    rows_half = NJ * NZ * RP // 2
    index = perm_ref[:, pl.ds(pl.multiple_of(x * SQ, SQ), SQ)]
    row_z = index >> log2(SP * NJ)
    row_j = ((index >> log2(SP)) - pair) & (NJ - 1)
    row_r = (index >> 7) & (RP - 1)
    row_of = (row_j * NZ + row_z) * RP + row_r
    lane_of = index & 127
    for h in range(2):
        for place in range(h * NJ // 2, (h + 1) * NJ // 2):

            def block_here(place=place):
                arrived_one("j", table.at[place], sem_ej, (pair + place) % NJ)

            if place < 2:
                pl.when(core != place)(block_here)
            else:
                block_here()
        flat = table[h * NJ // 2 : (h + 1) * NJ // 2].reshape(rows_half, 128)
        high, mid, low = split3(flat.T)
        tparts[0:128, :] = high
        tparts[128:256, :] = mid
        tparts[256:384, :] = low
        for c in range(SQ // W):
            cols = slice(c * W, (c + 1) * W)
            for b in range(8):
                hit = lax.broadcasted_iota(jnp.int32, (rows_half, W), 0) == row_of[b : b + 1, cols] - h * rows_half
                onehot = jnp.where(hit, 1.0, 0.0).astype(BF16)
                picked = sum3(jnp.dot(tparts[...], onehot, preferred_element_type=F32))
                lane_hit = lax.broadcasted_iota(jnp.int32, (128, W), 0) == lane_of[b : b + 1, cols]
                found = jnp.sum(jnp.where(lane_hit, picked, 0.0), axis=0, keepdims=True)
                if h == 0:
                    shuf[x, c, b : b + 1] = found
                else:
                    shuf[x, c, b : b + 1] = shuf[x, c, b : b + 1] + found
            if h == 1:
                each_peer("x", lambda peer, c=c: push("x", shuf.at[x, c], shuf.at[x, c], sem_sh.at[c], peer))

    lax.fori_loop(0, tchunks, tconvert, 0)
    for c in range(SQ // W):
        arrived("x", lambda peer, c=c: shuf.at[peer, c], sem_sh.at[c])

    def stacked(value_of, q):
        for c in range(SQ // W):
            value = value_of(q * SQ + c * W)
            parts_of = split3(jnp.concatenate([value, shuf[q, c] * value], axis=0))
            for k, part in enumerate(parts_of):
                parts[16 * k : 16 * k + 16, q * SQ + c * W : q * SQ + (c + 1) * W] = part

    for q in range(NX):
        stacked(lambda start: dir_ref[:, start : start + W], q)

    def product(block):
        cols = pl.ds(pl.multiple_of(block * VB, VB), VB)
        return sum3(jnp.dot(parts[...], gbf[:, cols], preferred_element_type=F32))

    def product_step(peer):
        psend[peer] = product(peer)
        push("j", psend.at[peer], precv.at[j], sem_p, peer)

    each_peer("j", product_step)
    precv[j] = product(j)

    for q in range(NX):
        stacked(lambda start: res_ref[:, start : start + W], q)
    apart = sum3(jnp.dot(parts[...], tbf[...], preferred_element_type=F32))
    quarters = TV // 128
    for i in range(NJ):
        h, q = divmod(i, quarters)
        asend[i] = apart[8 * h : 8 * h + 8, 128 * q : 128 * q + 128]

    arrived("j", lambda peer: precv.at[peer], sem_p)
    total = precv[0]
    for i in range(1, NJ):
        total = total + precv[i]
    pz[z] = total
    each_peer("z", lambda peer: push("z", pz.at[z], pz.at[z], sem_pz, peer))
    each_peer("j", lambda peer: push("j", asend.at[peer], arecv.at[j], sem_a, peer))
    arecv[j] = asend[j]
    arrived("z", lambda peer: pz.at[peer], sem_pz)
    total = pz[0]
    for i in range(1, NZ):
        total = total + pz[i]
    pall[j] = total
    each_peer("j", lambda peer: push("j", pall.at[j], pall.at[j], sem_pa, peer))

    def halves(first, place):
        for k in range(2):
            block = first + k
            for i, part in enumerate(split3(pall[block] * squares[block])):
                lefts[place, 16 * i : 16 * i + 16, k * VB : (k + 1) * VB] = part

    def against(place, rows, first):
        cols = pl.ds(pl.multiple_of(first * VB, 2 * VB), 2 * VB)
        return lax.dot_general(lefts[place], gbf[rows, cols], (((1,), (1,)), ((), ())), preferred_element_type=F32)

    other = pair + 1 - core
    arrived_one("j", pall.at[other], sem_pa, other)
    halves(pair, 0)
    acc[...] = sum3(against(0, slice(0, SP), pair))
    firsts = [(pair + 2 * k) % NJ for k in range(1, NJ // 2)]
    for first in firsts:
        for k in range(2):
            arrived_one("j", pall.at[first + k], sem_pa, first + k)
    for k, first in enumerate(firsts):
        halves(first, k + 1)

    def part_step(q, carry):
        rows = pl.ds(pl.multiple_of(q * SQ, SQ), SQ)
        value = acc[:, rows]
        if firsts:
            total = against(1, rows, firsts[0])
            for k in range(1, len(firsts)):
                total = total + against(k + 1, rows, firsts[k])
            value = value + sum3(total)
        for c in range(SQ // W):
            cols = slice(c * W, (c + 1) * W)
            isend[q, :, cols] = (
                vc_ref[1] * value[0:8, cols] + vc_ref[2] * shuf[q, c] * value[8:16, cols]
            ) * (1.0 / scale_rows)
        each_peer("x", lambda peer: push("x", isend.at[q], irecv.at[x, q], sem_im.at[q], peer))
        irecv[x, q] = isend[q]
        return carry

    lax.fori_loop(0, NX, part_step, 0)

    sent("z", lambda peer: expo_ref, sem_ez)
    sent("j", lambda peer: table.at[core], sem_ej)
    for c in range(SQ // W):
        sent("x", lambda peer, c=c: shuf.at[x, c], sem_sh.at[c])
    sent("j", lambda peer: psend.at[peer], sem_p)
    sent("z", lambda peer: pz.at[z], sem_pz)
    sent("j", lambda peer: pall.at[j], sem_pa)
    sent("j", lambda peer: asend.at[peer], sem_a)
    arrived("j", lambda peer: arecv.at[peer], sem_a)
    asum = arecv[0]
    for i in range(1, NJ):
        asum = asum + arecv[i]
    sums = [jnp.zeros((8, 1), F32) for _ in range(4)]
    bpart = None
    images = []
    for q in range(NX):
        cols = slice(q * SQ, (q + 1) * SQ)
        arrived("x", lambda peer, q=q: irecv.at[peer, q], sem_im.at[q])
        image = irecv[0, q]
        for i in range(1, NX):
            image = image + irecv[i, q]
        d, r = dir_ref[:, cols], res_ref[:, cols]
        image = vc_ref[0] * d + image
        images.append(image)
        stacked(lambda start, q=q, image=image: image[:, start - q * SQ : start - q * SQ + W], q)
        value = sum3(jnp.dot(parts[:, cols], tbf[cols, :], preferred_element_type=F32))
        bpart = value if bpart is None else bpart + value
        for k, term in enumerate((r * r, d * image, r * image, image * image)):
            sums[k] = sums[k] + jnp.sum(term, axis=1, keepdims=True)
    lane = lax.broadcasted_iota(jnp.int32, (8, 128), 1)
    scalars = jnp.where(lane == 0, sums[0], jnp.where(lane == 1, sums[1], jnp.where(lane == 2, sums[2], sums[3])))
    for i in range(NJ):
        h, q = divmod(i, quarters)
        fsend[i, 0] = bpart[8 * h : 8 * h + 8, 128 * q : 128 * q + 128]
        fsend[i, 1] = scalars
    each_peer("j", lambda peer: push("j", fsend.at[peer], frecv.at[j], sem_f, peer))
    frecv[j] = fsend[j]
    for q in range(NX):
        sent("x", lambda peer, q=q: isend.at[q], sem_im.at[q])
    for q in range(NX):
        isend[q] = images[q]
    arrived("j", lambda peer: frecv.at[peer], sem_f)
    total = frecv[0]
    for i in range(1, NJ):
        total = total + frecv[i]
    fz[z, 0] = asum
    fz[z, 1] = total[0]
    fz[z, 2] = total[1]
    each_peer("z", lambda peer: push("z", fz.at[z], fz.at[z], sem_fz, peer))
    sent("j", lambda peer: fsend.at[peer], sem_f)
    arrived("z", lambda peer: fz.at[peer], sem_fz)
    total = fz[0]
    for i in range(1, NZ):
        total = total + fz[i]
    norm_now = total[2][:, 0:1]
    curvature = total[2][:, 1:2]
    alpha = norm_now / curvature
    fall[j] = total[0] - alpha * total[1]
    each_peer("j", lambda peer: push("j", fall.at[j], fall.at[j], sem_fa, peer))

    norm_next = norm_now - 2.0 * alpha * total[2][:, 2:3] + alpha * alpha * total[2][:, 3:4]
    beta = norm_next / norm_now
    for q in range(NX):
        cols = slice(q * SQ, (q + 1) * SQ)
        d = dir_ref[:, cols]
        new_res = res_ref[:, cols] - alpha * isend[q]
        osol_ref[:, cols] = sol_ref[:, cols] + alpha * d
        ores_ref[:, cols] = new_res
        odir_ref[:, cols] = new_res + beta * d
    sent("z", lambda peer: fz.at[z], sem_fz)

    tfreq = tpct / 100.0
    root = float(NZ * NJ * SP) ** 0.5 * 50.0
    tscale = lax.rsqrt(2.0 * tfreq * (1.0 - tfreq)) / root
    arrived("j", lambda peer: fall.at[peer], sem_fa)
    for i in range(NJ):
        h, q = divmod(i, quarters)
        cols = slice(128 * q, 128 * q + 128)
        oassoc_ref[8 * h : 8 * h + 8, cols] = fall[i] * tscale[:, cols]
    sent("j", lambda peer: fall.at[j], sem_fa)


def local(dims, geno, allele_pct, test_geno, test_pct, exposure, perm, var_comp, solution, resid, direction):
    NZ, NJ, NX, _ = dims
    SP, V = geno.shape
    TV = test_geno.shape[1]
    RP, VB, SQ = SP // 128, V // NJ, SP // NX
    W = min(SQ, 256)
    chunks, tchunks = 8, 2
    vmem = pl.BlockSpec(memory_space=pltpu.VMEM)
    hbm = pl.BlockSpec(memory_space=pltpu.HBM)
    dma = pltpu.SemaphoreType.DMA
    rhs = jax.ShapeDtypeStruct((8, SP), F32)
    outs = (rhs, rhs, rhs, jax.ShapeDtypeStruct((16, TV), F32))
    results = pl.pallas_call(
        functools.partial(kernel, dims),
        out_shape=outs,
        in_specs=[hbm] * 10,
        out_specs=(vmem, vmem, vmem, vmem),
        scratch_shapes=[
            pltpu.SMEM((3,), F32),
            pltpu.VMEM((RP, 128), F32),
            pltpu.VMEM((8, SP), jnp.int32),
            pltpu.VMEM((1, V), jnp.int32),
            pltpu.VMEM((1, TV), jnp.int32),
            pltpu.VMEM((8, SP), F32),
            pltpu.VMEM((8, SP), F32),
            pltpu.VMEM((8, SP), F32),
            pltpu.VMEM((chunks, SP // chunks, V), jnp.int32),
            pltpu.VMEM((tchunks, SP // tchunks, TV), jnp.int32),
            pltpu.VMEM((SP, V), BF16),
            pltpu.VMEM((SP, TV), BF16),
            pltpu.VMEM((NJ, NZ, RP, 128), F32),
            pltpu.VMEM((384, NJ * NZ * RP // 2), BF16),
            pltpu.VMEM((NX, SQ // W, 8, W), F32),
            pltpu.VMEM((48, max(SP, V)), BF16),
            pltpu.VMEM((NJ // 2, 48, 2 * VB), BF16),
            pltpu.VMEM((NJ, 1, VB), F32),
            pltpu.VMEM((16, SP), F32),
            pltpu.VMEM((NJ, 16, VB), F32),
            pltpu.VMEM((NJ, 16, VB), F32),
            pltpu.VMEM((NZ, 16, VB), F32),
            pltpu.VMEM((NJ, 16, VB), F32),
            pltpu.VMEM((NJ, 8, 128), F32),
            pltpu.VMEM((NJ, 8, 128), F32),
            pltpu.VMEM((NX, NX, 8, SQ), F32),
            pltpu.VMEM((NX, 8, SQ), F32),
            pltpu.VMEM((NJ, 2, 8, 128), F32),
            pltpu.VMEM((NJ, 2, 8, 128), F32),
            pltpu.VMEM((NZ, 3, 8, 128), F32),
            pltpu.VMEM((NJ, 8, 128), F32),
            dma((8,)),
            dma((chunks,)),
            dma((tchunks,)),
            dma((2, NZ)),
            dma((2, NJ)),
            dma((SQ // W, 2, NX)),
            dma((2, NJ)),
            dma((2, NZ)),
            dma((2, NJ)),
            dma((2, NJ)),
            dma((NX, 2, NX)),
            dma((2, NJ)),
            dma((2, NZ)),
            dma((2, NJ)),
        ],
        compiler_params=pltpu.CompilerParams(
            collective_id=0, has_side_effects=True, vmem_limit_bytes=40 * 1024 * 1024
        ),
    )(
        *(
            pltpu.with_memory_space_constraint(value, pltpu.HBM)
            for value in (
                geno,
                test_geno,
                allele_pct.reshape(1, V),
                test_pct.reshape(1, TV),
                exposure.reshape(RP, 128),
                perm,
                var_comp,
                solution,
                resid,
                direction,
            )
        )
    )
    return pl.pallas_call(
        hand_over,
        out_shape=outs,
        in_specs=[vmem] * 4,
        out_specs=(vmem,) * 4,
        compiler_params=pltpu.CompilerParams(vmem_limit_bytes=2 * 1024 * 1024),
    )(*results)


def hand_over(*refs):
    for source, target in zip(refs[:4], refs[4:]):
        target[...] = source[...]


def solution(mesh):
    samp, var = mesh.shape["samp"], mesh.shape["var"]
    near = 8 if samp == 32 else samp // 2

    def whole(geno, *rest):
        dims = (samp // near, near, var, float(geno.shape[1]))
        return jax.shard_map(
            functools.partial(local, dims),
            mesh=mesh,
            in_specs=(
                P("samp", "var"),
                P("var"),
                P("samp", "var"),
                P("var"),
                P("samp"),
                P(None, "samp"),
                P(),
                P(None, "samp"),
                P(None, "samp"),
                P(None, "samp"),
            ),
            out_specs=(P(None, "samp"), P(None, "samp"), P(None, "samp"), P(None, "var")),
            check_vma=False,
        )(geno, *rest)

    return whole
```

time: 64.8 us -> 53.2 us (0.82)
  local copies, waits for them, and re-layouts: 5.79 us -> 0 us
  Pallas kernels: 58 us -> 52.4 us
    unnamed x4 -> x0, local copies, waits for them, and re-layouts: 5.79 us -> none
    pallas_call x1 -> x2, Pallas kernels: 58 us -> 52.4 us  [the longest x1 51.7 us: local(): pl.pallas_call(functools.partial(kernel, dims), out_shape=outs, in_specs=...]
where the time goes in v2:
time: 53.2 us; the launch traced here: 53 us
  Pallas kernels  52.4 us (98%)
  between operations  0.64 us (1%)
    pallas_call x1, Pallas kernels, local(): pl.pallas_call(functools.partial(kernel, dims), out_shape=outs, in_specs=...  51.7 us

profile of v2, /device:TPU:1, one launch (start us, length us, event | category | flops | bytes accessed | tf_op | source)
XLA Modules:
  0.0 53.0 jit_solution(9326973757450533734)
XLA Ops:
  0.6 51.7 %shard_map.129 = (f32[8,2048]{1,0:T(8,128)S(1)}, f32[8,2048]{1,0:T(8,128)S(1)}, f32[8,2048]{1,0:T(8,128)S(1)}, f32[16,512]{1,0:T(8,128)S(1)}) custom-call(s32[2048,2048]{1,0:T(8,128)} %geno_hbm.1, s32[2048,512]{1,0:T(8,128)} %tgeno_hbm.1, s32[1,2048]{1,0:T(1,128)} %bitcast.3, s32[1,512]{1,0:T(1,128)} %bitcast.5, f32[16,128]{1,0:T(8,128)} %bitcast.4, ...), custom_call_target="tpu_custom_call" | custom-call | tf_op jit(solution)/shard_map/pallas_call | solution.py:405
  52.4 0.7 %shard_map.130 = (f32[8,2048]{1,0:T(8,128)}, f32[8,2048]{1,0:T(8,128)}, f32[8,2048]{1,0:T(8,128)}, f32[16,512]{1,0:T(8,128)}) custom-call(f32[8,2048]{1,0:T(8,128)S(1)} %get-tuple-element.8.refs_0_, f32[8,2048]{1,0:T(8,128)S(1)} %get-tuple-element.9.refs_1_, f32[8,2048]{1,0:T(8,128)S(1)} %get-tuple-element.10.refs_2_, f32[16,512]{1,0:T(8,128)S(1)} %get-tuple-element.11.refs_3_), custom_call_target="tpu_custom_call" | custom-call | tf_op jit(solution)/shard_map/pallas_call | solution.py:477

commit v3 on v2

v3 whole, which is shorter than its diff:
```python
import functools

import jax
import jax.numpy as jnp
from jax import lax
from jax.experimental import pallas as pl
from jax.experimental.pallas import tpu as pltpu
from jax.sharding import PartitionSpec as P

MESH = pl.DeviceIdType.MESH
F32 = jnp.float32
BF16 = jnp.bfloat16


def log2(n):
    return n.bit_length() - 1


def split3(value):
    high = value.astype(BF16)
    rest = value - high.astype(F32)
    mid = rest.astype(BF16)
    low = (rest - mid.astype(F32)).astype(BF16)
    return high, mid, low


def sum3(value):
    rows = value.shape[0] // 3
    return value[:rows] + value[rows : 2 * rows] + value[2 * rows :]


def kernel(
    dims,
    geno_hbm, tgeno_hbm, pct_hbm, tpct_hbm, expo_hbm, perm_hbm, vc_hbm, sol_hbm, res_hbm, dir_hbm,
    osol_ref, ores_ref, odir_ref, oassoc_ref,
    vc_ref, perm_ref, pct_ref, tpct_ref, sol_ref, res_ref, dir_ref,
    graw, traw, gbf, tbf, table, tparts, row_of, lane_of, shuf, parts, lefts, squares, acc, image_ref, apart, bpart,
    psend, precv, pz, pall, asend, arecv, aall, irecv, isend, fsend, frecv, fall, sums_z,
    isem, gsem, tsem, sem_ez, sem_ej, sem_sh, sem_p, sem_pz, sem_pa, sem_a, sem_aa, sem_im, sem_f, sem_fa, sem_sz,
):
    NZ, NJ, NX, scale_rows = dims
    NY, NS = NJ // 2, NZ * NJ
    samp = lax.axis_index("samp")
    x = lax.axis_index("var")
    z = samp // NJ
    j = samp % NJ
    core = j % 2
    pair = j - core
    SP = dir_ref.shape[1]
    V = pct_ref.shape[1]
    TV = tpct_ref.shape[1]
    RP = SP // 128
    VB = V // NJ
    SQ = SP // NX
    W = min(SQ, 256)
    CW = SQ // W
    quarters = TV // 128
    chunks = graw.shape[0]
    crows = graw.shape[1]
    tchunks = traw.shape[0]
    trows = traw.shape[1]

    def loop(count, body):
        def step(i, carry):
            body(i)
            return carry

        lax.fori_loop(0, count, step, 0)

    def block(i, size):
        return pl.ds(pl.multiple_of(i * size, size), size)

    reads = [
        pltpu.make_async_copy(src, dst, isem.at[i])
        for i, (src, dst) in enumerate((
            (expo_hbm, table.at[core, z]), (pct_hbm, pct_ref), (perm_hbm, perm_ref), (dir_hbm, dir_ref),
            (res_hbm, res_ref), (tpct_hbm, tpct_ref), (sol_hbm, sol_ref), (vc_hbm, vc_ref),
        ))
    ]

    def gread(i):
        return pltpu.make_async_copy(geno_hbm.at[pl.ds(i * crows, crows), :], graw.at[i], gsem.at[i])

    def tread(i):
        return pltpu.make_async_copy(tgeno_hbm.at[pl.ds(i * trows, trows), :], traw.at[i], tsem.at[i])

    def outward(t, count):
        return (count // 2 + ((t + 1) // 2) * (2 * (t % 2) - 1)) % count

    def to_near(peer):
        return {"samp": z * NJ + peer}

    def nth_near(t):
        side = (core + t % 2 + t // (NJ - 2)) % 2
        return (pair + 2 * outward(t // 2, NY)) % NJ + side

    def to_z(peer):
        return {"samp": peer * NJ + j}

    def nth_z(t):
        return (z + outward(t, NZ)) % NZ

    def to_x(peer):
        return {"var": peer}

    def nth_x(t):
        return (x + outward(t, NX)) % NX

    def to_any(peer):
        return {"samp": peer}

    def nth_any(t):
        return (samp + NS // 2) % NS

    near = (NJ, nth_near, to_near)
    over_z = (NZ, nth_z, to_z)
    over_x = (NX, nth_x, to_x)
    everyone = (NS, nth_any, to_any)

    def each_peer(group, body, rolled=False):
        count, nth, _ = group
        if group is not everyone:
            if rolled:
                loop(count - 1, lambda t: body(nth(t)))
            else:
                for t in range(count - 1):
                    body(nth(t))
            return

        def plane(t):
            first = (z + outward(t, NZ)) % NZ * NJ
            for k in range(NY):
                chip = first + (pair + 2 * outward(k, NY)) % NJ
                body(chip + 1 - core)
                if k < NY - 1:
                    body(chip + core)
                else:
                    pl.when(t < NZ - 1)(lambda chip=chip: body(chip + core))

        loop(NZ, plane)

    def push(group, src, dst, sem, peer, arrival=1):
        pltpu.make_async_remote_copy(
            src_ref=src, dst_ref=dst, send_sem=sem.at[0], recv_sem=sem.at[arrival],
            device_id=group[2](peer), device_id_type=MESH,
        ).start()

    def described(group, like, sem, arrival):
        return pltpu.make_async_remote_copy(
            src_ref=like, dst_ref=like, send_sem=sem.at[0], recv_sem=sem.at[arrival],
            device_id=group[2](group[1](0)), device_id_type=MESH,
        )

    def arrived(group, like, sem, arrival=1):
        described(group, like, sem, arrival).wait_recv()

    def sent(group, like, sem):
        described(group, like, sem, 1).wait_send()

    barrier = pltpu.get_barrier_semaphore()
    reads[0].start()
    for group in (near, over_z, over_x):
        each_peer(
            group,
            lambda peer, group=group: pl.semaphore_signal(
                barrier, inc=1, device_id=group[2](peer), device_id_type=MESH
            ),
        )
    for copy in reads[1:]:
        copy.start()
    loop(chunks, lambda i: gread(i).start())
    loop(tchunks, lambda i: tread(i).start())
    pl.semaphore_wait(barrier, NJ + NZ + NX - 3)

    each_peer(over_z, lambda peer: push(over_z, expo_hbm, table.at[core, z], sem_ez, peer))

    reads[1].wait()
    reads[5].wait()
    pct = pct_ref[...].astype(F32)
    tpct = tpct_ref[...].astype(F32)

    def convert(i):
        gread(i).wait()

        def rows(r):
            codes = graw[i, block(r, 32), :].astype(F32)
            gbf[block(i * (crows // 32) + r, 32), :] = (codes * 50.0 - pct).astype(BF16)

        loop(crows // 32, rows)

    def tconvert(i):
        tread(i).wait()

        def rows(r):
            codes = traw[i, block(r, 64), :].astype(F32)
            tbf[block(i * (trows // 64) + r, 64), :] = (codes * 50.0 - tpct).astype(BF16)

        loop(trows // 64, rows)

    loop(chunks // 2, convert)

    reads[0].wait()
    arrived(over_z, table.at[0, pl.ds(0, NZ - 1)], sem_ez)

    def share(peer):
        place = (j - (peer - peer % 2) + NJ) % NJ
        push(near, table.at[core], table.at[place], sem_ej, peer, 1 + place // NY)

    each_peer(near, share)

    loop(chunks - chunks // 2, lambda i: convert(chunks // 2 + i))
    freq = pct / 100.0
    square = 1.0 / (2.0 * freq * (1.0 - freq)) / 2500.0
    for i in range(NJ):
        squares[i] = square[:, i * VB : (i + 1) * VB]
    for i in (2, 3, 4, 6, 7):
        reads[i].wait()

    rows_half = NS * RP // 2
    index = perm_ref[:, block(x, SQ)]
    index_z = index >> log2(SP * NJ)
    index_j = ((index >> log2(SP)) - pair) & (NJ - 1)
    index_r = (index >> 7) & (RP - 1)
    row = (index_j * NZ + index_z) * RP + index_r
    for b in range(8):
        row_of[b] = row[b : b + 1]
        lane_of[b] = index[b : b + 1] & 127
    sublane = lax.broadcasted_iota(jnp.int32, (8, W), 0)
    deep = lax.broadcasted_iota(jnp.int32, (rows_half, W), 0)
    lanes = lax.broadcasted_iota(jnp.int32, (128, W), 0)
    for h in range(2):
        arrived(near, table.at[pl.ds(0, NY - 1 + h)], sem_ej, 1 + h)
        flat = table[h * NY : (h + 1) * NY].reshape(rows_half, 128)
        for k, part in enumerate(split3(flat.T)):
            tparts[128 * k : 128 * k + 128, :] = part

        def lookup(c, h=h):
            cols = block(c, W)

            found = jnp.zeros((8, W), F32)
            for b in range(8):
                onehot = jnp.where(deep == row_of[b, :, cols] - h * rows_half, 1.0, 0.0).astype(BF16)
                picked = sum3(jnp.dot(tparts[...], onehot, preferred_element_type=F32))
                value = jnp.sum(jnp.where(lanes == lane_of[b, :, cols], picked, 0.0), axis=0, keepdims=True)
                found = jnp.where(sublane == b, value, found)
            mine = x * CW + c
            if h == 0:
                shuf[mine] = found
            else:
                shuf[mine] = shuf[mine] + found
                each_peer(over_x, lambda peer: push(over_x, shuf.at[mine], shuf.at[mine], sem_sh, peer))

        loop(CW, lookup)

    loop(tchunks, tconvert)
    arrived(over_x, shuf.at[pl.ds(0, CW * (NX - 1))], sem_sh)

    def stack(value, i):
        for k, part in enumerate(split3(jnp.concatenate([value, shuf[i] * value], axis=0))):
            parts[16 * k : 16 * k + 16, block(i, W)] = part

    loop(SP // W, lambda i: stack(dir_ref[:, block(i, W)], i))

    def product(target, place, t):
        target[place] = sum3(jnp.dot(parts[...], gbf[:, block(t, VB)], preferred_element_type=F32))

    def product_step(peer):
        product(psend, peer, peer)
        push(near, psend.at[peer], precv.at[j], sem_p, peer)

    each_peer(near, product_step, rolled=True)
    product(precv, j, j)

    loop(SP // W, lambda i: stack(res_ref[:, block(i, W)], i))
    TW = min(TV, 256)

    def ascore(i):
        cols = block(i, TW)
        apart[:, cols] = sum3(jnp.dot(parts[...], tbf[:, cols], preferred_element_type=F32))

    loop(TV // TW, ascore)
    spots = []
    for i in range(NJ):
        h, q = divmod(i, quarters)
        spots.append((slice(8 * h, 8 * h + 8), slice(128 * q, 128 * q + 128)))
    for i, spot in enumerate(spots):
        asend[i] = apart[spot]

    arrived(near, precv.at[pl.ds(0, NJ - 1)], sem_p)
    total = precv[0]
    for i in range(1, NJ):
        total = total + precv[i]
    pz[z] = total
    each_peer(over_z, lambda peer: push(over_z, pz.at[z], pz.at[z], sem_pz, peer))
    each_peer(near, lambda peer: push(near, asend.at[peer], arecv.at[j], sem_a, peer))
    arecv[j] = asend[j]
    arrived(over_z, pz.at[pl.ds(0, NZ - 1)], sem_pz)
    total = pz[0]
    for i in range(1, NZ):
        total = total + pz[i]
    pall[j] = total

    def share_sum(peer):
        other = (peer - peer % 2 - pair + NJ) % NJ
        push(near, pall.at[j], pall.at[j], sem_pa, peer, 1 + (other + NJ - 1) // NJ)

    each_peer(near, share_sum)

    def halves(first, place):
        for k in range(2):
            for i, part in enumerate(split3(pall[first + k] * squares[first + k])):
                lefts[place, 16 * i : 16 * i + 16, k * VB : (k + 1) * VB] = part

    def against(place, rows, first):
        cols = pl.ds(pl.multiple_of(first * VB, 2 * VB), 2 * VB)
        return lax.dot_general(lefts[place], gbf[rows, cols], (((1,), (1,)), ((), ())), preferred_element_type=F32)

    arrived(near, pall.at[0], sem_pa, 1)
    halves(pair, 0)

    def own_part(q):
        acc[q] = against(0, block(q, SQ), pair)

    loop(NX, own_part)
    arrived(near, arecv.at[pl.ds(0, NJ - 1)], sem_a)
    total = arecv[0]
    for i in range(1, NJ):
        total = total + arecv[i]
    aall[samp] = total
    each_peer(everyone, lambda peer: push(everyone, aall.at[samp], aall.at[samp], sem_aa, peer))
    arrived(near, pall.at[pl.ds(0, NJ - 2)], sem_pa, 2)
    firsts = [(pair + 2 * k) % NJ for k in range(1, NY)]
    loop(NY - 1, lambda k: halves((pair + 2 * (k + 1)) % NJ, k + 1))

    def part_step(q):
        total = acc[q]
        for k, first in enumerate(firsts):
            total = total + against(k + 1, block(q, SQ), first)
        value = sum3(total)
        for c in range(CW):
            cols = slice(c * W, (c + 1) * W)
            isend[q, :, cols] = (
                vc_ref[1] * value[0:8, cols] + vc_ref[2] * shuf[q * CW + c] * value[8:16, cols]
            ) * (1.0 / scale_rows)
        each_peer(over_x, lambda peer: push(over_x, isend.at[q], irecv.at[q, x], sem_im.at[q], peer))
        irecv[q, x] = isend[q]

    loop(NX, part_step)

    sent(over_z, table.at[0, pl.ds(0, NZ - 1)], sem_ez)
    sent(near, table.at[pl.ds(0, NJ - 1)], sem_ej)
    sent(over_x, shuf.at[pl.ds(0, CW * (NX - 1))], sem_sh)
    sent(near, psend.at[pl.ds(0, NJ - 1)], sem_p)
    sent(over_z, pz.at[pl.ds(0, NZ - 1)], sem_pz)
    sent(near, pall.at[pl.ds(0, NJ - 1)], sem_pa)
    sent(near, asend.at[pl.ds(0, NJ - 1)], sem_a)
    sent(everyone, aall.at[pl.ds(0, NS - 1)], sem_aa)
    arrived(everyone, aall.at[pl.ds(0, NS - 1)], sem_aa)
    for i, spot in enumerate(spots):
        total = aall[i]
        for k in range(1, NZ):
            total = total + aall[k * NJ + i]
        apart[spot] = total
    bpart[...] = jnp.zeros_like(bpart)

    def score(q, sums):
        arrived(over_x, irecv.at[q, pl.ds(0, NX - 1)], sem_im.at[q])
        image = irecv[q, 0]
        for i in range(1, NX):
            image = image + irecv[q, i]
        cols = block(q, SQ)
        d, r = dir_ref[:, cols], res_ref[:, cols]
        image = vc_ref[0] * d + image
        image_ref[:, cols] = image
        for c in range(CW):
            stack(image[:, c * W : (c + 1) * W], q * CW + c)
        bpart[...] += sum3(jnp.dot(parts[:, cols], tbf[cols, :], preferred_element_type=F32))
        sums = list(sums)
        for k, term in enumerate((r * r, d * image, r * image, image * image)):
            for c in range(SQ // 128):
                sums[k] = sums[k] + term[:, 128 * c : 128 * c + 128]
        return tuple(sums)

    sums = lax.fori_loop(0, NX, score, (jnp.zeros((8, 128), F32),) * 4)
    lane = lax.broadcasted_iota(jnp.int32, (8, 128), 1) - lax.broadcasted_iota(jnp.int32, (8, 128), 0)
    scalars = jnp.zeros((8, 128), F32)
    for k in range(4):
        scalars = jnp.where(lane == 8 * k, jnp.sum(sums[k], axis=1, keepdims=True), scalars)
    scalars = jnp.broadcast_to(jnp.sum(scalars, axis=0, keepdims=True), (8, 128))
    for i, spot in enumerate(spots):
        fsend[i, 0] = bpart[spot]
        fsend[i, 1] = scalars
    each_peer(near, lambda peer: push(near, fsend.at[peer], frecv.at[j], sem_f, peer))
    frecv[j] = fsend[j]
    for q in range(NX):
        sent(over_x, isend.at[pl.ds(0, NX - 1)], sem_im.at[q])
    arrived(near, frecv.at[pl.ds(0, NJ - 1)], sem_f)
    total = frecv[0]
    for i in range(1, NJ):
        total = total + frecv[i]
    fall[samp] = total[0]
    sums_z[z] = total[1]
    each_peer(everyone, lambda peer: push(everyone, fall.at[samp], fall.at[samp], sem_fa, peer))
    each_peer(over_z, lambda peer: push(over_z, sums_z.at[z], sums_z.at[z], sem_sz, peer))
    arrived(over_z, sums_z.at[pl.ds(0, NZ - 1)], sem_sz)
    row = sums_z[0]
    for i in range(1, NZ):
        row = row + sums_z[i]
    norm_now, curvature, cross, square = (
        jnp.sum(jnp.where(lane == 8 * k, row, 0.0), axis=1, keepdims=True) for k in range(4)
    )
    alpha = norm_now / curvature

    norm_next = norm_now - 2.0 * alpha * cross + alpha * alpha * square
    beta = norm_next / norm_now
    d = dir_ref[...]
    new_res = res_ref[...] - alpha * image_ref[...]
    osol_ref[...] = sol_ref[...] + alpha * d
    ores_ref[...] = new_res
    odir_ref[...] = new_res + beta * d
    sent(near, fsend.at[pl.ds(0, NJ - 1)], sem_f)
    sent(over_z, sums_z.at[pl.ds(0, NZ - 1)], sem_sz)

    tfreq = tpct / 100.0
    root = float(NS * SP) ** 0.5 * 50.0
    tscale = lax.rsqrt(2.0 * tfreq * (1.0 - tfreq)) / root
    arrived(everyone, fall.at[pl.ds(0, NS - 1)], sem_fa)
    for i, spot in enumerate(spots):
        total = fall[i]
        for k in range(1, NZ):
            total = total + fall[k * NJ + i]
        oassoc_ref[spot] = (apart[spot] - alpha * total) * tscale[:, spot[1]]
    sent(everyone, fall.at[pl.ds(0, NS - 1)], sem_fa)


def local(dims, geno, allele_pct, test_geno, test_pct, exposure, perm, var_comp, solution, resid, direction):
    NZ, NJ, NX, _ = dims
    SP, V = geno.shape
    TV = test_geno.shape[1]
    RP, VB, SQ = SP // 128, V // NJ, SP // NX
    W = min(SQ, 256)
    chunks, tchunks = 4, 1
    NS = NZ * NJ
    vmem = pl.BlockSpec(memory_space=pltpu.VMEM)
    hbm = pl.BlockSpec(memory_space=pltpu.HBM)
    dma = pltpu.SemaphoreType.DMA
    rhs = jax.ShapeDtypeStruct((8, SP), F32)
    outs = (rhs, rhs, rhs, jax.ShapeDtypeStruct((16, TV), F32))
    results = pl.pallas_call(
        functools.partial(kernel, dims),
        out_shape=outs,
        in_specs=[hbm] * 10,
        out_specs=(vmem, vmem, vmem, vmem),
        scratch_shapes=[
            pltpu.SMEM((3,), F32),
            pltpu.VMEM((8, SP), jnp.int32),
            pltpu.VMEM((1, V), jnp.int32),
            pltpu.VMEM((1, TV), jnp.int32),
            pltpu.VMEM((8, SP), F32),
            pltpu.VMEM((8, SP), F32),
            pltpu.VMEM((8, SP), F32),
            pltpu.VMEM((chunks, SP // chunks, V), jnp.int32),
            pltpu.VMEM((tchunks, SP // tchunks, TV), jnp.int32),
            pltpu.VMEM((SP, V), BF16),
            pltpu.VMEM((SP, TV), BF16),
            pltpu.VMEM((NJ, NZ, RP, 128), F32),
            pltpu.VMEM((384, NS * RP // 2), BF16),
            pltpu.VMEM((8, 1, SQ), jnp.int32),
            pltpu.VMEM((8, 1, SQ), jnp.int32),
            pltpu.VMEM((SP // W, 8, W), F32),
            pltpu.VMEM((48, SP), BF16),
            pltpu.VMEM((NJ // 2, 48, 2 * VB), BF16),
            pltpu.VMEM((NJ, 1, VB), F32),
            pltpu.VMEM((NX, 48, SQ), F32),
            pltpu.VMEM((8, SP), F32),
            pltpu.VMEM((16, TV), F32),
            pltpu.VMEM((16, TV), F32),
            pltpu.VMEM((NJ, 16, VB), F32),
            pltpu.VMEM((NJ, 16, VB), F32),
            pltpu.VMEM((NZ, 16, VB), F32),
            pltpu.VMEM((NJ, 16, VB), F32),
            pltpu.VMEM((NJ, 8, 128), F32),
            pltpu.VMEM((NJ, 8, 128), F32),
            pltpu.VMEM((NS, 8, 128), F32),
            pltpu.VMEM((NX, NX, 8, SQ), F32),
            pltpu.VMEM((NX, 8, SQ), F32),
            pltpu.VMEM((NJ, 2, 8, 128), F32),
            pltpu.VMEM((NJ, 2, 8, 128), F32),
            pltpu.VMEM((NS, 8, 128), F32),
            pltpu.VMEM((NZ, 8, 128), F32),
            dma((8,)),
            dma((chunks,)),
            dma((tchunks,)),
            dma((2,)),
            dma((3,)),
            dma((2,)),
            dma((2,)),
            dma((2,)),
            dma((3,)),
            dma((2,)),
            dma((2,)),
            dma((NX, 2)),
            dma((2,)),
            dma((2,)),
            dma((2,)),
        ],
        compiler_params=pltpu.CompilerParams(
            collective_id=0, has_side_effects=True, vmem_limit_bytes=40 * 1024 * 1024
        ),
    )(
        *(
            pltpu.with_memory_space_constraint(value, pltpu.HBM)
            for value in (
                geno,
                test_geno,
                allele_pct.reshape(1, V),
                test_pct.reshape(1, TV),
                exposure.reshape(RP, 128),
                perm,
                var_comp,
                solution,
                resid,
                direction,
            )
        )
    )
    return pl.pallas_call(
        hand_over,
        out_shape=outs,
        in_specs=[vmem] * 4,
        out_specs=(vmem,) * 4,
        compiler_params=pltpu.CompilerParams(vmem_limit_bytes=2 * 1024 * 1024),
    )(*results)


def hand_over(*refs):
    for source, target in zip(refs[:4], refs[4:]):
        target[...] = source[...]


def solution(mesh):
    samp, var = mesh.shape["samp"], mesh.shape["var"]
    near = 8 if samp == 32 else samp // 2

    def whole(geno, *rest):
        dims = (samp // near, near, var, float(geno.shape[1]))
        return jax.shard_map(
            functools.partial(local, dims),
            mesh=mesh,
            in_specs=(
                P("samp", "var"),
                P("var"),
                P("samp", "var"),
                P("var"),
                P("samp"),
                P(None, "samp"),
                P(),
                P(None, "samp"),
                P(None, "samp"),
                P(None, "samp"),
            ),
            out_specs=(P(None, "samp"), P(None, "samp"), P(None, "samp"), P(None, "var")),
            check_vma=False,
        )(geno, *rest)

    return whole
```

time: 53.2 us -> 49.9 us (0.938)
  Pallas kernels: 52.4 us -> 49.2 us
    pallas_call x1, Pallas kernels: 51.7 us -> 48.5 us  [local(): pl.pallas_call(functools.partial(kernel, dims), out_shape=outs, in_specs=...]
where the time goes in v3:
time: 49.9 us; the launch traced here: 49.8 us
  Pallas kernels  49.2 us (99%)
  between operations  0.64 us (1%)
    pallas_call x1, Pallas kernels, local(): pl.pallas_call(functools.partial(kernel, dims), out_shape=outs, in_specs=...  48.5 us

profile of v3, /device:TPU:1, one launch (start us, length us, event | category | flops | bytes accessed | tf_op | source)
XLA Modules:
  0.0 49.8 jit_solution(4384685764622985598)
XLA Ops:
  0.6 48.5 %shard_map.129 = (f32[8,2048]{1,0:T(8,128)S(1)}, f32[8,2048]{1,0:T(8,128)S(1)}, f32[8,2048]{1,0:T(8,128)S(1)}, f32[16,512]{1,0:T(8,128)S(1)}) custom-call(s32[2048,2048]{1,0:T(8,128)} %geno_hbm.1, s32[2048,512]{1,0:T(8,128)} %tgeno_hbm.1, s32[1,2048]{1,0:T(1,128)} %bitcast.3, s32[1,512]{1,0:T(1,128)} %bitcast.5, f32[16,128]{1,0:T(8,128)} %bitcast.4, ...), custom_call_target="tpu_custom_call" | custom-call | tf_op jit(solution)/shard_map/pallas_call | solution.py:449
  49.1 0.7 %shard_map.130 = (f32[8,2048]{1,0:T(8,128)}, f32[8,2048]{1,0:T(8,128)}, f32[8,2048]{1,0:T(8,128)}, f32[16,512]{1,0:T(8,128)}) custom-call(f32[8,2048]{1,0:T(8,128)S(1)} %get-tuple-element.8.refs_0_, f32[8,2048]{1,0:T(8,128)S(1)} %get-tuple-element.9.refs_1_, f32[8,2048]{1,0:T(8,128)S(1)} %get-tuple-element.10.refs_2_, f32[16,512]{1,0:T(8,128)S(1)} %get-tuple-element.11.refs_3_), custom_call_target="tpu_custom_call" | custom-call | tf_op jit(solution)/shard_map/pallas_call | solution.py:527

commit v4 on v3

--- a/solution.py
+++ b/solution.py
@@ -34,9 +34,9 @@
     geno_hbm, tgeno_hbm, pct_hbm, tpct_hbm, expo_hbm, perm_hbm, vc_hbm, sol_hbm, res_hbm, dir_hbm,
     osol_ref, ores_ref, odir_ref, oassoc_ref,
     vc_ref, perm_ref, pct_ref, tpct_ref, sol_ref, res_ref, dir_ref,
-    graw, traw, gbf, tbf, table, tparts, row_of, lane_of, shuf, parts, lefts, squares, acc, image_ref, apart, bpart,
-    psend, precv, pz, pall, asend, arecv, aall, irecv, isend, fsend, frecv, fall, sums_z,
-    isem, gsem, tsem, sem_ez, sem_ej, sem_sh, sem_p, sem_pz, sem_pa, sem_a, sem_aa, sem_im, sem_f, sem_fa, sem_sz,
+    graw, traw, gbf, tbf, table, tparts, row_of, lane_of, shuf, parts, lefts, squares, pacc, acc, image_ref, apart, bpart,
+    psend, precv, pz, pall, asend, arecv, az, aall, irecv, isend, fsend, frecv, fall, sums_z,
+    isem, gsem, tsem, sem_ez, sem_ej, sem_sh, sem_p, sem_pz, sem_pa, sem_a, sem_az, sem_aa, sem_im, sem_f, sem_fa, sem_sz,
 ):
     NZ, NJ, NX, scale_rows = dims
     NY, NS = NJ // 2, NZ * NJ
@@ -46,6 +46,7 @@
     j = samp % NJ
     core = j % 2
     pair = j - core
+    y = j // 2
     SP = dir_ref.shape[1]
     V = pct_ref.shape[1]
     TV = tpct_ref.shape[1]
@@ -73,7 +74,7 @@
     reads = [
         pltpu.make_async_copy(src, dst, isem.at[i])
         for i, (src, dst) in enumerate((
-            (expo_hbm, table.at[core, z]), (pct_hbm, pct_ref), (perm_hbm, perm_ref), (dir_hbm, dir_ref),
+            (expo_hbm, table.at[core]), (pct_hbm, pct_ref), (perm_hbm, perm_ref), (dir_hbm, dir_ref),
             (res_hbm, res_ref), (tpct_hbm, tpct_ref), (sol_hbm, sol_ref), (vc_hbm, vc_ref),
         ))
     ]
@@ -111,6 +112,9 @@
 
     def nth_any(t):
         return (samp + NS // 2) % NS
+
+    def device(dz, dy, side):
+        return (z + dz) % NZ * NJ + (y + dy) % NY * 2 + side
 
     near = (NJ, nth_near, to_near)
     over_z = (NZ, nth_z, to_z)
@@ -166,13 +170,23 @@
                 barrier, inc=1, device_id=group[2](peer), device_id_type=MESH
             ),
         )
+    for side in range(2):
+        pl.semaphore_signal(barrier, inc=1, device_id=to_any(device(1, 1, side)), device_id_type=MESH)
     for copy in reads[1:]:
         copy.start()
     loop(chunks, lambda i: gread(i).start())
     loop(tchunks, lambda i: tread(i).start())
-    pl.semaphore_wait(barrier, NJ + NZ + NX - 3)
-
-    each_peer(over_z, lambda peer: push(over_z, expo_hbm, table.at[core, z], sem_ez, peer))
+    pl.semaphore_wait(barrier, NJ + NZ + NX - 1)
+
+    layers = 2 * NY + 3 * core
+    each_peer(
+        over_z, lambda peer: push(over_z, expo_hbm, table.at[layers + (z - peer + NZ) % NZ - 1], sem_ez, peer)
+    )
+    each_peer(
+        near, lambda peer: push(near, expo_hbm, table.at[(j - (peer - peer % 2) + NJ) % NJ], sem_ej, peer)
+    )
+    for side in range(2):
+        push(everyone, expo_hbm, table.at[14 + core], sem_ej, device(NZ - 1, NY - 1, side))
 
     reads[1].wait()
     reads[5].wait()
@@ -200,13 +214,16 @@
     loop(chunks // 2, convert)
 
     reads[0].wait()
-    arrived(over_z, table.at[0, pl.ds(0, NZ - 1)], sem_ez)
-
-    def share(peer):
-        place = (j - (peer - peer % 2) + NJ) % NJ
-        push(near, table.at[core], table.at[place], sem_ej, peer, 1 + place // NY)
-
-    each_peer(near, share)
+    arrived(over_z, table.at[pl.ds(0, NZ - 1)], sem_ez)
+
+    push(near, table.at[pl.ds(layers, 3)], table.at[pl.ds(layers, 3)], sem_ej, pair + 1 - core)
+    for dy, skip, start in ((2, 0, 20), (1, 1, 16), (3, 0, 26)):
+        size = 3 - skip
+        for side in range(2):
+            push(
+                everyone, table.at[pl.ds(layers + skip, size)], table.at[pl.ds(start + size * core, size)],
+                sem_ej, device(0, NY - dy, side), 2,
+            )
 
     loop(chunks - chunks // 2, lambda i: convert(chunks // 2 + i))
     freq = pct / 100.0
@@ -218,10 +235,13 @@
 
     rows_half = NS * RP // 2
     index = perm_ref[:, block(x, SQ)]
-    index_z = index >> log2(SP * NJ)
-    index_j = ((index >> log2(SP)) - pair) & (NJ - 1)
-    index_r = (index >> 7) & (RP - 1)
-    row = (index_j * NZ + index_z) * RP + index_r
+    dz = ((index >> log2(SP * NJ)) - z) & (NZ - 1)
+    dy = ((index >> log2(2 * SP)) - y) & (NY - 1)
+    side = (index >> log2(SP)) & 1
+    early = jnp.where(dz == 0, 2 * dy + side, jnp.where(dy == 0, 7 + 3 * side + dz, 14 + side))
+    late = jnp.where(dy == 1, 14 + 2 * side + dz, jnp.where(dy == 2, 19, 25) + 3 * side + dz)
+    place = jnp.where((dz == 0) | (dy == 0) | ((dz == 1) & (dy == 1)), early, late)
+    row = place * RP + ((index >> 7) & (RP - 1))
     for b in range(8):
         row_of[b] = row[b : b + 1]
         lane_of[b] = index[b : b + 1] & 127
@@ -229,8 +249,8 @@
     deep = lax.broadcasted_iota(jnp.int32, (rows_half, W), 0)
     lanes = lax.broadcasted_iota(jnp.int32, (128, W), 0)
     for h in range(2):
-        arrived(near, table.at[pl.ds(0, NY - 1 + h)], sem_ej, 1 + h)
-        flat = table[h * NY : (h + 1) * NY].reshape(rows_half, 128)
+        arrived(near, table.at[pl.ds(0, 12 + 4 * h)], sem_ej, 1 + h)
+        flat = table[16 * h : 16 * h + 16].reshape(rows_half, 128)
         for k, part in enumerate(split3(flat.T)):
             tparts[128 * k : 128 * k + 128, :] = part
 
@@ -252,24 +272,45 @@
 
         loop(CW, lookup)
 
-    loop(tchunks, tconvert)
-    arrived(over_x, shuf.at[pl.ds(0, CW * (NX - 1))], sem_sh)
 
     def stack(value, i):
         for k, part in enumerate(split3(jnp.concatenate([value, shuf[i] * value], axis=0))):
             parts[16 * k : 16 * k + 16, block(i, W)] = part
 
-    loop(SP // W, lambda i: stack(dir_ref[:, block(i, W)], i))
-
-    def product(target, place, t):
-        target[place] = sum3(jnp.dot(parts[...], gbf[:, block(t, VB)], preferred_element_type=F32))
-
-    def product_step(peer):
-        product(psend, peer, peer)
+    def stack_dir(i):
+        stack(dir_ref[:, block(i, W)], i)
+
+    def on_part(q, t):
+        return jnp.dot(parts[:, block(q, SQ)], gbf[block(q, SQ), block(t, VB)], preferred_element_type=F32)
+
+    loop(CW, lambda i: stack_dir(x * CW + i))
+
+    def own_products(i):
+        for t in (2 * i, 2 * i + 1):
+            pacc[t] = on_part(x, t)
+
+    loop(NJ // 2, own_products)
+    loop(tchunks, tconvert)
+    arrived(over_x, shuf.at[pl.ds(0, CW * (NX - 1))], sem_sh)
+    loop(CW * (NX - 1), lambda i: stack_dir((x * CW + CW + i) % (NX * CW)))
+
+    def product(peer):
+        total = pacc[peer]
+        for k in range(1, NX):
+            total = total + on_part((x + k) % NX, peer)
+        psend[peer] = sum3(total)
+
+    def give(peer):
         push(near, psend.at[peer], precv.at[j], sem_p, peer)
 
-    each_peer(near, product_step, rolled=True)
-    product(precv, j, j)
+    def two_products(i):
+        product(nth_near(2 * i))
+        product(nth_near(2 * i + 1))
+        give(nth_near(2 * i))
+        pl.when(i < NJ // 2 - 1)(lambda: give(nth_near(2 * i + 1)))
+
+    loop(NJ // 2, two_products)
+    precv[j] = psend[j]
 
     loop(SP // W, lambda i: stack(res_ref[:, block(i, W)], i))
     TW = min(TV, 256)
@@ -306,6 +347,12 @@
 
     each_peer(near, share_sum)
 
+    arrived(near, arecv.at[pl.ds(0, NJ - 1)], sem_a)
+    total = arecv[0]
+    for i in range(1, NJ):
+        total = total + arecv[i]
+    az[z] = total
+    each_peer(over_z, lambda peer: push(over_z, az.at[z], az.at[z], sem_az, peer))
     def halves(first, place):
         for k in range(2):
             for i, part in enumerate(split3(pall[first + k] * squares[first + k])):
@@ -322,12 +369,6 @@
         acc[q] = against(0, block(q, SQ), pair)
 
     loop(NX, own_part)
-    arrived(near, arecv.at[pl.ds(0, NJ - 1)], sem_a)
-    total = arecv[0]
-    for i in range(1, NJ):
-        total = total + arecv[i]
-    aall[samp] = total
-    each_peer(everyone, lambda peer: push(everyone, aall.at[samp], aall.at[samp], sem_aa, peer))
     arrived(near, pall.at[pl.ds(0, NJ - 2)], sem_pa, 2)
     firsts = [(pair + 2 * k) % NJ for k in range(1, NY)]
     loop(NY - 1, lambda k: halves((pair + 2 * (k + 1)) % NJ, k + 1))
@@ -347,20 +388,19 @@
 
     loop(NX, part_step)
 
-    sent(over_z, table.at[0, pl.ds(0, NZ - 1)], sem_ez)
-    sent(near, table.at[pl.ds(0, NJ - 1)], sem_ej)
+    arrived(over_z, az.at[pl.ds(0, NZ - 1)], sem_az)
+    total = az[0]
+    for i in range(1, NZ):
+        total = total + az[i]
+    aall[j] = total
+    each_peer(near, lambda peer: push(near, aall.at[j], aall.at[j], sem_aa, peer))
+    sent(over_z, table.at[pl.ds(0, NZ - 1)], sem_ez)
+    sent(near, table.at[pl.ds(0, 28)], sem_ej)
     sent(over_x, shuf.at[pl.ds(0, CW * (NX - 1))], sem_sh)
     sent(near, psend.at[pl.ds(0, NJ - 1)], sem_p)
     sent(over_z, pz.at[pl.ds(0, NZ - 1)], sem_pz)
     sent(near, pall.at[pl.ds(0, NJ - 1)], sem_pa)
     sent(near, asend.at[pl.ds(0, NJ - 1)], sem_a)
-    sent(everyone, aall.at[pl.ds(0, NS - 1)], sem_aa)
-    arrived(everyone, aall.at[pl.ds(0, NS - 1)], sem_aa)
-    for i, spot in enumerate(spots):
-        total = aall[i]
-        for k in range(1, NZ):
-            total = total + aall[k * NJ + i]
-        apart[spot] = total
     bpart[...] = jnp.zeros_like(bpart)
 
     def score(q, sums):
@@ -394,6 +434,9 @@
     frecv[j] = fsend[j]
     for q in range(NX):
         sent(over_x, isend.at[pl.ds(0, NX - 1)], sem_im.at[q])
+    sent(over_z, az.at[pl.ds(0, NZ - 1)], sem_az)
+    sent(near, aall.at[pl.ds(0, NJ - 1)], sem_aa)
+    arrived(near, aall.at[pl.ds(0, NJ - 1)], sem_aa)
     arrived(near, frecv.at[pl.ds(0, NJ - 1)], sem_f)
     total = frecv[0]
     for i in range(1, NJ):
@@ -429,7 +472,7 @@
         total = fall[i]
         for k in range(1, NZ):
             total = total + fall[k * NJ + i]
-        oassoc_ref[spot] = (apart[spot] - alpha * total) * tscale[:, spot[1]]
+        oassoc_ref[spot] = (aall[i] - alpha * total) * tscale[:, spot[1]]
     sent(everyone, fall.at[pl.ds(0, NS - 1)], sem_fa)
 
 
@@ -463,7 +506,7 @@
             pltpu.VMEM((tchunks, SP // tchunks, TV), jnp.int32),
             pltpu.VMEM((SP, V), BF16),
             pltpu.VMEM((SP, TV), BF16),
-            pltpu.VMEM((NJ, NZ, RP, 128), F32),
+            pltpu.VMEM((NS, RP, 128), F32),
             pltpu.VMEM((384, NS * RP // 2), BF16),
             pltpu.VMEM((8, 1, SQ), jnp.int32),
             pltpu.VMEM((8, 1, SQ), jnp.int32),
@@ -471,6 +514,7 @@
             pltpu.VMEM((48, SP), BF16),
             pltpu.VMEM((NJ // 2, 48, 2 * VB), BF16),
             pltpu.VMEM((NJ, 1, VB), F32),
+            pltpu.VMEM((NJ, 48, VB), F32),
             pltpu.VMEM((NX, 48, SQ), F32),
             pltpu.VMEM((8, SP), F32),
             pltpu.VMEM((16, TV), F32),
@@ -481,7 +525,8 @@
             pltpu.VMEM((NJ, 16, VB), F32),
             pltpu.VMEM((NJ, 8, 128), F32),
             pltpu.VMEM((NJ, 8, 128), F32),
-            pltpu.VMEM((NS, 8, 128), F32),
+            pltpu.VMEM((NZ, 8, 128), F32),
+            pltpu.VMEM((NJ, 8, 128), F32),
             pltpu.VMEM((NX, NX, 8, SQ), F32),
             pltpu.VMEM((NX, 8, SQ), F32),
             pltpu.VMEM((NJ, 2, 8, 128), F32),
@@ -497,6 +542,7 @@
             dma((2,)),
             dma((2,)),
             dma((3,)),
+            dma((2,)),
             dma((2,)),
             dma((2,)),
             dma((NX, 2)),

time: 49.9 us -> 48.1 us (0.964)
  Pallas kernels: 49.2 us -> 47.4 us
    pallas_call x1, Pallas kernels: 48.5 us -> 46.7 us  [local(): pl.pallas_call(functools.partial(kernel, dims), out_shape=outs, in_specs=...]
where the time goes in v4:
time: 48.1 us; the launch traced here: 48 us
  Pallas kernels  47.4 us (99%)
  between operations  0.64 us (1%)
    pallas_call x1, Pallas kernels, local(): pl.pallas_call(functools.partial(kernel, dims), out_shape=outs, in_specs=...  46.7 us

profile of v4, /device:TPU:1, one launch (start us, length us, event | category | flops | bytes accessed | tf_op | source)
XLA Modules:
  0.0 48.0 jit_solution(18158125335051427350)
XLA Ops:
  0.6 46.7 %shard_map.129 = (f32[8,2048]{1,0:T(8,128)S(1)}, f32[8,2048]{1,0:T(8,128)S(1)}, f32[8,2048]{1,0:T(8,128)S(1)}, f32[16,512]{1,0:T(8,128)S(1)}) custom-call(s32[2048,2048]{1,0:T(8,128)} %geno_hbm.1, s32[2048,512]{1,0:T(8,128)} %tgeno_hbm.1, s32[1,2048]{1,0:T(1,128)} %bitcast.3, s32[1,512]{1,0:T(1,128)} %bitcast.5, f32[16,128]{1,0:T(8,128)} %bitcast.4, ...), custom_call_target="tpu_custom_call" | custom-call | tf_op jit(solution)/shard_map/pallas_call | solution.py:492
  47.3 0.7 %shard_map.130 = (f32[8,2048]{1,0:T(8,128)}, f32[8,2048]{1,0:T(8,128)}, f32[8,2048]{1,0:T(8,128)}, f32[16,512]{1,0:T(8,128)}) custom-call(f32[8,2048]{1,0:T(8,128)S(1)} %get-tuple-element.8.refs_0_, f32[8,2048]{1,0:T(8,128)S(1)} %get-tuple-element.9.refs_1_, f32[8,2048]{1,0:T(8,128)S(1)} %get-tuple-element.10.refs_2_, f32[16,512]{1,0:T(8,128)S(1)} %get-tuple-element.11.refs_3_), custom_call_target="tpu_custom_call" | custom-call | tf_op jit(solution)/shard_map/pallas_call | solution.py:573

commit v5 on v4

--- a/solution.py
+++ b/solution.py
@@ -35,8 +35,8 @@
     osol_ref, ores_ref, odir_ref, oassoc_ref,
     vc_ref, perm_ref, pct_ref, tpct_ref, sol_ref, res_ref, dir_ref,
     graw, traw, gbf, tbf, table, tparts, row_of, lane_of, shuf, parts, lefts, squares, pacc, acc, image_ref, apart, bpart,
-    psend, precv, pz, pall, asend, arecv, az, aall, irecv, isend, fsend, frecv, fall, sums_z,
-    isem, gsem, tsem, sem_ez, sem_ej, sem_sh, sem_p, sem_pz, sem_pa, sem_a, sem_az, sem_aa, sem_im, sem_f, sem_fa, sem_sz,
+    psend, precv, pall, asend, arecv, az, aall, irecv, isend, fsend, frecv, fall, sums_z,
+    isem, gsem, tsem, sem_ez, sem_ej, sem_sh, sem_p, sem_pa, sem_a, sem_az, sem_aa, sem_im, sem_f, sem_fa, sem_sz,
 ):
     NZ, NJ, NX, scale_rows = dims
     NY, NS = NJ // 2, NZ * NJ
@@ -51,7 +51,7 @@
     V = pct_ref.shape[1]
     TV = tpct_ref.shape[1]
     RP = SP // 128
-    VB = V // NJ
+    VB, VZ = V // NJ, V // NZ
     SQ = SP // NX
     W = min(SQ, 256)
     CW = SQ // W
@@ -131,17 +131,17 @@
                     body(nth(t))
             return
 
-        def plane(t):
-            first = (z + outward(t, NZ)) % NZ * NJ
-            for k in range(NY):
-                chip = first + (pair + 2 * outward(k, NY)) % NJ
-                body(chip + 1 - core)
-                if k < NY - 1:
-                    body(chip + core)
-                else:
-                    pl.when(t < NZ - 1)(lambda chip=chip: body(chip + core))
-
-        loop(NZ, plane)
+        loop(NZ, lambda t: each_in_plane(t, body))
+
+    def each_in_plane(t, body):
+        first = (z + outward(t, NZ)) % NZ * NJ
+        for k in range(NY):
+            chip = first + (pair + 2 * outward(k, NY)) % NJ
+            body(chip + 1 - core)
+            if k < NY - 1:
+                body(chip + core)
+            else:
+                pl.when(t < NZ - 1)(lambda chip=chip: body(chip + core))
 
     def push(group, src, dst, sem, peer, arrival=1):
         pltpu.make_async_remote_copy(
@@ -182,9 +182,9 @@
     each_peer(
         over_z, lambda peer: push(over_z, expo_hbm, table.at[layers + (z - peer + NZ) % NZ - 1], sem_ez, peer)
     )
-    each_peer(
-        near, lambda peer: push(near, expo_hbm, table.at[(j - (peer - peer % 2) + NJ) % NJ], sem_ej, peer)
-    )
+    for dy in (2, 1, 3, 0):
+        for side in (1 - core, core)[: 1 if dy == 0 else 2]:
+            push(everyone, expo_hbm, table.at[2 * dy + core], sem_ej, device(0, NY - dy, side), 3 if dy == 2 else 1)
     for side in range(2):
         push(everyone, expo_hbm, table.at[14 + core], sem_ej, device(NZ - 1, NY - 1, side))
 
@@ -217,19 +217,26 @@
     arrived(over_z, table.at[pl.ds(0, NZ - 1)], sem_ez)
 
     push(near, table.at[pl.ds(layers, 3)], table.at[pl.ds(layers, 3)], sem_ej, pair + 1 - core)
-    for dy, skip, start in ((2, 0, 20), (1, 1, 16), (3, 0, 26)):
+    for dy, skip, start in ((3, 0, 26), (1, 1, 16)):
         size = 3 - skip
         for side in range(2):
             push(
                 everyone, table.at[pl.ds(layers + skip, size)], table.at[pl.ds(start + size * core, size)],
                 sem_ej, device(0, NY - dy, side), 2,
             )
+    arrived(near, table.at[pl.ds(0, 2)], sem_ej, 3)
+    each_peer(
+        over_z,
+        lambda peer: push(
+            over_z, table.at[pl.ds(4, 2)], table.at[pl.ds(18 + 2 * ((z - peer + NZ) % NZ), 2)], sem_ej, peer, 2
+        ),
+    )
 
     loop(chunks - chunks // 2, lambda i: convert(chunks // 2 + i))
     freq = pct / 100.0
     square = 1.0 / (2.0 * freq * (1.0 - freq)) / 2500.0
-    for i in range(NJ):
-        squares[i] = square[:, i * VB : (i + 1) * VB]
+    for i in range(V // 128):
+        squares[i] = square[:, i * 128 : (i + 1) * 128]
     for i in (2, 3, 4, 6, 7):
         reads[i].wait()
 
@@ -239,7 +246,7 @@
     dy = ((index >> log2(2 * SP)) - y) & (NY - 1)
     side = (index >> log2(SP)) & 1
     early = jnp.where(dz == 0, 2 * dy + side, jnp.where(dy == 0, 7 + 3 * side + dz, 14 + side))
-    late = jnp.where(dy == 1, 14 + 2 * side + dz, jnp.where(dy == 2, 19, 25) + 3 * side + dz)
+    late = jnp.where(dy == 1, 14 + 2 * side + dz, jnp.where(dy == 2, 18 + 2 * dz + side, 25 + 3 * side + dz))
     place = jnp.where((dz == 0) | (dy == 0) | ((dz == 1) & (dy == 1)), early, late)
     row = place * RP + ((index >> 7) & (RP - 1))
     for b in range(8):
@@ -249,7 +256,7 @@
     deep = lax.broadcasted_iota(jnp.int32, (rows_half, W), 0)
     lanes = lax.broadcasted_iota(jnp.int32, (128, W), 0)
     for h in range(2):
-        arrived(near, table.at[pl.ds(0, 12 + 4 * h)], sem_ej, 1 + h)
+        arrived(near, table.at[pl.ds(0, 10 + 6 * h)], sem_ej, 1 + h)
         flat = table[16 * h : 16 * h + 16].reshape(rows_half, 128)
         for k, part in enumerate(split3(flat.T)):
             tparts[128 * k : 128 * k + 128, :] = part
@@ -294,23 +301,24 @@
     arrived(over_x, shuf.at[pl.ds(0, CW * (NX - 1))], sem_sh)
     loop(CW * (NX - 1), lambda i: stack_dir((x * CW + CW + i) % (NX * CW)))
 
-    def product(peer):
-        total = pacc[peer]
+    def product(layer, half):
+        t = layer * (VZ // VB) + half
+        total = pacc[t]
         for k in range(1, NX):
-            total = total + on_part((x + k) % NX, peer)
-        psend[peer] = sum3(total)
-
-    def give(peer):
-        push(near, psend.at[peer], precv.at[j], sem_p, peer)
-
-    def two_products(i):
-        product(nth_near(2 * i))
-        product(nth_near(2 * i + 1))
-        give(nth_near(2 * i))
-        pl.when(i < NJ // 2 - 1)(lambda: give(nth_near(2 * i + 1)))
-
-    loop(NJ // 2, two_products)
-    precv[j] = psend[j]
+            total = total + on_part((x + k) % NX, t)
+        total = sum3(total)
+        for k in range(VB // 128):
+            for h in range(2):
+                owner = layer * NJ + 2 * (half * (VB // 128) + k) + h
+                psend[owner] = total[8 * h : 8 * h + 8, 128 * k : 128 * k + 128]
+
+    def layer_step(t):
+        for half in range(VZ // VB):
+            product((z + outward(t, NZ)) % NZ, half)
+        each_in_plane(t, lambda peer: push(everyone, psend.at[peer], precv.at[samp], sem_p, peer))
+
+    loop(NZ, layer_step)
+    precv[samp] = psend[samp]
 
     loop(SP // W, lambda i: stack(res_ref[:, block(i, W)], i))
     TW = min(TV, 256)
@@ -326,26 +334,19 @@
         spots.append((slice(8 * h, 8 * h + 8), slice(128 * q, 128 * q + 128)))
     for i, spot in enumerate(spots):
         asend[i] = apart[spot]
-
-    arrived(near, precv.at[pl.ds(0, NJ - 1)], sem_p)
-    total = precv[0]
-    for i in range(1, NJ):
-        total = total + precv[i]
-    pz[z] = total
-    each_peer(over_z, lambda peer: push(over_z, pz.at[z], pz.at[z], sem_pz, peer))
     each_peer(near, lambda peer: push(near, asend.at[peer], arecv.at[j], sem_a, peer))
     arecv[j] = asend[j]
-    arrived(over_z, pz.at[pl.ds(0, NZ - 1)], sem_pz)
-    total = pz[0]
-    for i in range(1, NZ):
-        total = total + pz[i]
-    pall[j] = total
-
-    def share_sum(peer):
-        other = (peer - peer % 2 - pair + NJ) % NJ
-        push(near, pall.at[j], pall.at[j], sem_pa, peer, 1 + (other + NJ - 1) // NJ)
-
-    each_peer(near, share_sum)
+
+    arrived(everyone, precv.at[pl.ds(0, NS - 1)], sem_p)
+    total = precv[0]
+    for i in range(1, NS):
+        total = total + precv[i]
+    pall[samp] = total
+
+    def share_sums(t):
+        each_in_plane(t, lambda peer: push(everyone, pall.at[samp], pall.at[samp], sem_pa, peer, 2 - t // (NZ - 1)))
+
+    loop(NZ, share_sums)
 
     arrived(near, arecv.at[pl.ds(0, NJ - 1)], sem_a)
     total = arecv[0]
@@ -353,30 +354,33 @@
         total = total + arecv[i]
     az[z] = total
     each_peer(over_z, lambda peer: push(over_z, az.at[z], az.at[z], sem_az, peer))
-    def halves(first, place):
-        for k in range(2):
-            for i, part in enumerate(split3(pall[first + k] * squares[first + k])):
-                lefts[place, 16 * i : 16 * i + 16, k * VB : (k + 1) * VB] = part
-
-    def against(place, rows, first):
-        cols = pl.ds(pl.multiple_of(first * VB, 2 * VB), 2 * VB)
-        return lax.dot_general(lefts[place], gbf[rows, cols], (((1,), (1,)), ((), ())), preferred_element_type=F32)
-
-    arrived(near, pall.at[0], sem_pa, 1)
-    halves(pair, 0)
-
-    def own_part(q):
-        acc[q] = against(0, block(q, SQ), pair)
-
-    loop(NX, own_part)
-    arrived(near, pall.at[pl.ds(0, NJ - 2)], sem_pa, 2)
-    firsts = [(pair + 2 * k) % NJ for k in range(1, NY)]
-    loop(NY - 1, lambda k: halves((pair + 2 * (k + 1)) % NJ, k + 1))
-
-    def part_step(q):
+    def scaled(layer, place):
+        for k in range(NY):
+            chip = layer * NY + k
+            sums = jnp.concatenate([pall[2 * chip], pall[2 * chip + 1]], axis=0) * squares[chip]
+            for i, part in enumerate(split3(sums)):
+                lefts[place, 16 * i : 16 * i + 16, k * 128 : (k + 1) * 128] = part
+
+    def against(place, rows):
+        return lax.dot_general(
+            lefts[place], gbf[rows, block((z + place) % NZ, VZ)], (((1,), (1,)), ((), ())), preferred_element_type=F32
+        )
+
+    arrived(everyone, pall.at[pl.ds(0, NJ - 1)], sem_pa, 1)
+    scaled(z, 0)
+
+    def own_parts(i):
+        for q in (2 * i, 2 * i + 1):
+            acc[q] = against(0, block(q, SQ))
+
+    loop(NX // 2, own_parts)
+    arrived(everyone, pall.at[pl.ds(0, NS - NJ)], sem_pa, 2)
+    loop(NZ - 1, lambda k: scaled((z + k + 1) % NZ, k + 1))
+
+    def part(q):
         total = acc[q]
-        for k, first in enumerate(firsts):
-            total = total + against(k + 1, block(q, SQ), first)
+        for k in range(1, NZ):
+            total = total + against(k, block(q, SQ))
         value = sum3(total)
         for c in range(CW):
             cols = slice(c * W, (c + 1) * W)
@@ -386,7 +390,7 @@
         each_peer(over_x, lambda peer: push(over_x, isend.at[q], irecv.at[q, x], sem_im.at[q], peer))
         irecv[q, x] = isend[q]
 
-    loop(NX, part_step)
+    loop(NX, part)
 
     arrived(over_z, az.at[pl.ds(0, NZ - 1)], sem_az)
     total = az[0]
@@ -397,9 +401,8 @@
     sent(over_z, table.at[pl.ds(0, NZ - 1)], sem_ez)
     sent(near, table.at[pl.ds(0, 28)], sem_ej)
     sent(over_x, shuf.at[pl.ds(0, CW * (NX - 1))], sem_sh)
-    sent(near, psend.at[pl.ds(0, NJ - 1)], sem_p)
-    sent(over_z, pz.at[pl.ds(0, NZ - 1)], sem_pz)
-    sent(near, pall.at[pl.ds(0, NJ - 1)], sem_pa)
+    sent(everyone, psend.at[pl.ds(0, NS - 1)], sem_p)
+    sent(everyone, pall.at[pl.ds(0, NS - 1)], sem_pa)
     sent(near, asend.at[pl.ds(0, NJ - 1)], sem_a)
     bpart[...] = jnp.zeros_like(bpart)
 
@@ -434,9 +437,6 @@
     frecv[j] = fsend[j]
     for q in range(NX):
         sent(over_x, isend.at[pl.ds(0, NX - 1)], sem_im.at[q])
-    sent(over_z, az.at[pl.ds(0, NZ - 1)], sem_az)
-    sent(near, aall.at[pl.ds(0, NJ - 1)], sem_aa)
-    arrived(near, aall.at[pl.ds(0, NJ - 1)], sem_aa)
     arrived(near, frecv.at[pl.ds(0, NJ - 1)], sem_f)
     total = frecv[0]
     for i in range(1, NJ):
@@ -468,6 +468,9 @@
     root = float(NS * SP) ** 0.5 * 50.0
     tscale = lax.rsqrt(2.0 * tfreq * (1.0 - tfreq)) / root
     arrived(everyone, fall.at[pl.ds(0, NS - 1)], sem_fa)
+    sent(over_z, az.at[pl.ds(0, NZ - 1)], sem_az)
+    sent(near, aall.at[pl.ds(0, NJ - 1)], sem_aa)
+    arrived(near, aall.at[pl.ds(0, NJ - 1)], sem_aa)
     for i, spot in enumerate(spots):
         total = fall[i]
         for k in range(1, NZ):
@@ -512,17 +515,16 @@
             pltpu.VMEM((8, 1, SQ), jnp.int32),
             pltpu.VMEM((SP // W, 8, W), F32),
             pltpu.VMEM((48, SP), BF16),
-            pltpu.VMEM((NJ // 2, 48, 2 * VB), BF16),
-            pltpu.VMEM((NJ, 1, VB), F32),
+            pltpu.VMEM((NZ, 48, V // NZ), BF16),
+            pltpu.VMEM((V // 128, 1, 128), F32),
             pltpu.VMEM((NJ, 48, VB), F32),
             pltpu.VMEM((NX, 48, SQ), F32),
             pltpu.VMEM((8, SP), F32),
             pltpu.VMEM((16, TV), F32),
             pltpu.VMEM((16, TV), F32),
-            pltpu.VMEM((NJ, 16, VB), F32),
-            pltpu.VMEM((NJ, 16, VB), F32),
-            pltpu.VMEM((NZ, 16, VB), F32),
-            pltpu.VMEM((NJ, 16, VB), F32),
+            pltpu.VMEM((NS, 8, 128), F32),
+            pltpu.VMEM((NS, 8, 128), F32),
+            pltpu.VMEM((NS, 8, 128), F32),
             pltpu.VMEM((NJ, 8, 128), F32),
             pltpu.VMEM((NJ, 8, 128), F32),
             pltpu.VMEM((NZ, 8, 128), F32),
@@ -537,8 +539,7 @@
             dma((chunks,)),
             dma((tchunks,)),
             dma((2,)),
-            dma((3,)),
-            dma((2,)),
+            dma((4,)),
             dma((2,)),
             dma((2,)),
             dma((3,)),

time: 48.1 us -> 47.2 us (0.981)
  Pallas kernels: 47.4 us -> 46.4 us
    pallas_call x1, Pallas kernels: 46.7 us -> 45.7 us  [local(): pl.pallas_call(functools.partial(kernel, dims), out_shape=outs, in_specs=...]
where the time goes in v5:
time: 47.2 us; the launch traced here: 47.1 us
  Pallas kernels  46.4 us (98%)
  between operations  0.64 us (1%)
    pallas_call x1, Pallas kernels, local(): pl.pallas_call(functools.partial(kernel, dims), out_shape=outs, in_specs=...  45.7 us

profile of v5, /device:TPU:1, one launch (start us, length us, event | category | flops | bytes accessed | tf_op | source)
XLA Modules:
  0.0 47.1 jit_solution(1647726124261349751)
XLA Ops:
  0.6 45.7 %shard_map.129 = (f32[8,2048]{1,0:T(8,128)S(1)}, f32[8,2048]{1,0:T(8,128)S(1)}, f32[8,2048]{1,0:T(8,128)S(1)}, f32[16,512]{1,0:T(8,128)S(1)}) custom-call(s32[2048,2048]{1,0:T(8,128)} %geno_hbm.1, s32[2048,512]{1,0:T(8,128)} %tgeno_hbm.1, s32[1,2048]{1,0:T(1,128)} %bitcast.3, s32[1,512]{1,0:T(1,128)} %bitcast.5, f32[16,128]{1,0:T(8,128)} %bitcast.4, ...), custom_call_target="tpu_custom_call" | custom-call | tf_op jit(solution)/shard_map/pallas_call | solution.py:495
  46.4 0.7 %shard_map.130 = (f32[8,2048]{1,0:T(8,128)}, f32[8,2048]{1,0:T(8,128)}, f32[8,2048]{1,0:T(8,128)}, f32[16,512]{1,0:T(8,128)}) custom-call(f32[8,2048]{1,0:T(8,128)S(1)} %get-tuple-element.8.refs_0_, f32[8,2048]{1,0:T(8,128)S(1)} %get-tuple-element.9.refs_1_, f32[8,2048]{1,0:T(8,128)S(1)} %get-tuple-element.10.refs_2_, f32[16,512]{1,0:T(8,128)S(1)} %get-tuple-element.11.refs_3_), custom_call_target="tpu_custom_call" | custom-call | tf_op jit(solution)/shard_map/pallas_call | solution.py:574

commit v6 on v5

--- a/solution.py
+++ b/solution.py
@@ -35,8 +35,8 @@
     osol_ref, ores_ref, odir_ref, oassoc_ref,
     vc_ref, perm_ref, pct_ref, tpct_ref, sol_ref, res_ref, dir_ref,
     graw, traw, gbf, tbf, table, tparts, row_of, lane_of, shuf, parts, lefts, squares, pacc, acc, image_ref, apart, bpart,
-    psend, precv, pall, asend, arecv, az, aall, irecv, isend, fsend, frecv, fall, sums_z,
-    isem, gsem, tsem, sem_ez, sem_ej, sem_sh, sem_p, sem_pa, sem_a, sem_az, sem_aa, sem_im, sem_f, sem_fa, sem_sz,
+    psend, precv, pall, asend, arecv, az, aall, irecv, isend, fsend, frecv, fall, srecv, sums_z,
+    isem, gsem, tsem, sem_ez, sem_ej, sem_sh, sem_p, sem_pa, sem_a, sem_az, sem_aa, sem_im, sem_f, sem_fa, sem_s, sem_sz,
 ):
     NZ, NJ, NX, scale_rows = dims
     NY, NS = NJ // 2, NZ * NJ
@@ -179,14 +179,16 @@
     pl.semaphore_wait(barrier, NJ + NZ + NX - 1)
 
     layers = 2 * NY + 3 * core
+    reads[0].wait()
+    mine = table.at[core]
     each_peer(
-        over_z, lambda peer: push(over_z, expo_hbm, table.at[layers + (z - peer + NZ) % NZ - 1], sem_ez, peer)
+        over_z, lambda peer: push(over_z, mine, table.at[layers + (z - peer + NZ) % NZ - 1], sem_ez, peer)
     )
     for dy in (2, 1, 3, 0):
         for side in (1 - core, core)[: 1 if dy == 0 else 2]:
-            push(everyone, expo_hbm, table.at[2 * dy + core], sem_ej, device(0, NY - dy, side), 3 if dy == 2 else 1)
+            push(everyone, mine, table.at[2 * dy + core], sem_ej, device(0, NY - dy, side), 3 if dy == 2 else 1)
     for side in range(2):
-        push(everyone, expo_hbm, table.at[14 + core], sem_ej, device(NZ - 1, NY - 1, side))
+        push(everyone, mine, table.at[14 + core], sem_ej, device(NZ - 1, NY - 1, side))
 
     reads[1].wait()
     reads[5].wait()
@@ -213,7 +215,6 @@
 
     loop(chunks // 2, convert)
 
-    reads[0].wait()
     arrived(over_z, table.at[pl.ds(0, NZ - 1)], sem_ez)
 
     push(near, table.at[pl.ds(layers, 3)], table.at[pl.ds(layers, 3)], sem_ej, pair + 1 - core)
@@ -270,12 +271,12 @@
                 picked = sum3(jnp.dot(tparts[...], onehot, preferred_element_type=F32))
                 value = jnp.sum(jnp.where(lanes == lane_of[b, :, cols], picked, 0.0), axis=0, keepdims=True)
                 found = jnp.where(sublane == b, value, found)
-            mine = x * CW + c
+            own = x * CW + c
             if h == 0:
-                shuf[mine] = found
+                shuf[own] = found
             else:
-                shuf[mine] = shuf[mine] + found
-                each_peer(over_x, lambda peer: push(over_x, shuf.at[mine], shuf.at[mine], sem_sh, peer))
+                shuf[own] = shuf[own] + found
+                each_peer(over_x, lambda peer: push(over_x, shuf.at[own], shuf.at[own], sem_sh, peer, (x - peer + NX) % NX))
 
         loop(CW, lookup)
 
@@ -298,8 +299,9 @@
 
     loop(NJ // 2, own_products)
     loop(tchunks, tconvert)
-    arrived(over_x, shuf.at[pl.ds(0, CW * (NX - 1))], sem_sh)
-    loop(CW * (NX - 1), lambda i: stack_dir((x * CW + CW + i) % (NX * CW)))
+    for k in sorted(range(1, NX), key=lambda k: min(k, NX - k)):
+        arrived(over_x, shuf.at[pl.ds(0, CW)], sem_sh, k)
+        loop(CW, lambda i, k=k: stack_dir((x + k) % NX * CW + i))
 
     def product(layer, half):
         t = layer * (VZ // VB) + half
@@ -344,9 +346,10 @@
     pall[samp] = total
 
     def share_sums(t):
-        each_in_plane(t, lambda peer: push(everyone, pall.at[samp], pall.at[samp], sem_pa, peer, 2 - t // (NZ - 1)))
-
-    loop(NZ, share_sums)
+        offset = (NZ - outward(t, NZ)) % NZ
+        each_in_plane(t, lambda peer: push(everyone, pall.at[samp], pall.at[samp], sem_pa, peer, 1 + offset))
+
+    loop(NZ, lambda i: share_sums(i * (NZ - 1) % NZ))
 
     arrived(near, arecv.at[pl.ds(0, NJ - 1)], sem_a)
     total = arecv[0]
@@ -374,8 +377,9 @@
             acc[q] = against(0, block(q, SQ))
 
     loop(NX // 2, own_parts)
-    arrived(everyone, pall.at[pl.ds(0, NS - NJ)], sem_pa, 2)
-    loop(NZ - 1, lambda k: scaled((z + k + 1) % NZ, k + 1))
+    for k in sorted(range(1, NZ), key=lambda k: min(k, NZ - k)):
+        arrived(everyone, pall.at[pl.ds(0, NJ)], sem_pa, 1 + k)
+        scaled((z + k) % NZ, k)
 
     def part(q):
         total = acc[q]
@@ -431,19 +435,24 @@
         scalars = jnp.where(lane == 8 * k, jnp.sum(sums[k], axis=1, keepdims=True), scalars)
     scalars = jnp.broadcast_to(jnp.sum(scalars, axis=0, keepdims=True), (8, 128))
     for i, spot in enumerate(spots):
-        fsend[i, 0] = bpart[spot]
-        fsend[i, 1] = scalars
+        fsend[i] = bpart[spot]
+    srecv[j] = scalars
     each_peer(near, lambda peer: push(near, fsend.at[peer], frecv.at[j], sem_f, peer))
     frecv[j] = fsend[j]
+    each_peer(near, lambda peer: push(near, srecv.at[j], srecv.at[j], sem_s, peer))
     for q in range(NX):
         sent(over_x, isend.at[pl.ds(0, NX - 1)], sem_im.at[q])
     arrived(near, frecv.at[pl.ds(0, NJ - 1)], sem_f)
     total = frecv[0]
     for i in range(1, NJ):
         total = total + frecv[i]
-    fall[samp] = total[0]
-    sums_z[z] = total[1]
+    fall[samp] = total
     each_peer(everyone, lambda peer: push(everyone, fall.at[samp], fall.at[samp], sem_fa, peer))
+    arrived(near, srecv.at[pl.ds(0, NJ - 1)], sem_s)
+    total = srecv[0]
+    for i in range(1, NJ):
+        total = total + srecv[i]
+    sums_z[z] = total
     each_peer(over_z, lambda peer: push(over_z, sums_z.at[z], sums_z.at[z], sem_sz, peer))
     arrived(over_z, sums_z.at[pl.ds(0, NZ - 1)], sem_sz)
     row = sums_z[0]
@@ -462,6 +471,7 @@
     ores_ref[...] = new_res
     odir_ref[...] = new_res + beta * d
     sent(near, fsend.at[pl.ds(0, NJ - 1)], sem_f)
+    sent(near, srecv.at[pl.ds(0, NJ - 1)], sem_s)
     sent(over_z, sums_z.at[pl.ds(0, NZ - 1)], sem_sz)
 
     tfreq = tpct / 100.0
@@ -531,22 +541,24 @@
             pltpu.VMEM((NJ, 8, 128), F32),
             pltpu.VMEM((NX, NX, 8, SQ), F32),
             pltpu.VMEM((NX, 8, SQ), F32),
-            pltpu.VMEM((NJ, 2, 8, 128), F32),
-            pltpu.VMEM((NJ, 2, 8, 128), F32),
+            pltpu.VMEM((NJ, 8, 128), F32),
+            pltpu.VMEM((NJ, 8, 128), F32),
             pltpu.VMEM((NS, 8, 128), F32),
+            pltpu.VMEM((NJ, 8, 128), F32),
             pltpu.VMEM((NZ, 8, 128), F32),
             dma((8,)),
             dma((chunks,)),
             dma((tchunks,)),
             dma((2,)),
             dma((4,)),
-            dma((2,)),
-            dma((2,)),
-            dma((3,)),
+            dma((NX,)),
+            dma((2,)),
+            dma((1 + NZ,)),
             dma((2,)),
             dma((2,)),
             dma((2,)),
             dma((NX, 2)),
+            dma((2,)),
             dma((2,)),
             dma((2,)),
             dma((2,)),

time: 47.2 us -> 47 us (level)
  no operation moved by 1% of the time
where the time goes in v6:
time: 47 us; the launch traced here: 46.9 us
  Pallas kernels  46.3 us (99%)
  between operations  0.64 us (1%)
    pallas_call x1, Pallas kernels, local(): pl.pallas_call(functools.partial(kernel, dims), out_shape=outs, in_specs=...  45.6 us

profile of v6, /device:TPU:1, one launch (start us, length us, event | category | flops | bytes accessed | tf_op | source)
XLA Modules:
  0.0 46.9 jit_solution(5479663335706001522)
XLA Ops:
  0.6 45.6 %shard_map.129 = (f32[8,2048]{1,0:T(8,128)S(1)}, f32[8,2048]{1,0:T(8,128)S(1)}, f32[8,2048]{1,0:T(8,128)S(1)}, f32[16,512]{1,0:T(8,128)S(1)}) custom-call(s32[2048,2048]{1,0:T(8,128)} %geno_hbm.1, s32[2048,512]{1,0:T(8,128)} %tgeno_hbm.1, s32[1,2048]{1,0:T(1,128)} %bitcast.3, s32[1,512]{1,0:T(1,128)} %bitcast.5, f32[16,128]{1,0:T(8,128)} %bitcast.4, ...), custom_call_target="tpu_custom_call" | custom-call | tf_op jit(solution)/shard_map/pallas_call | solution.py:505
  46.2 0.7 %shard_map.130 = (f32[8,2048]{1,0:T(8,128)}, f32[8,2048]{1,0:T(8,128)}, f32[8,2048]{1,0:T(8,128)}, f32[16,512]{1,0:T(8,128)}) custom-call(f32[8,2048]{1,0:T(8,128)S(1)} %get-tuple-element.8.refs_0_, f32[8,2048]{1,0:T(8,128)S(1)} %get-tuple-element.9.refs_1_, f32[8,2048]{1,0:T(8,128)S(1)} %get-tuple-element.10.refs_2_, f32[16,512]{1,0:T(8,128)S(1)} %get-tuple-element.11.refs_3_), custom_call_target="tpu_custom_call" | custom-call | tf_op jit(solution)/shard_map/pallas_call | solution.py:586

commit v7 on v5

--- a/solution.py
+++ b/solution.py
@@ -179,14 +179,16 @@
     pl.semaphore_wait(barrier, NJ + NZ + NX - 1)
 
     layers = 2 * NY + 3 * core
+    reads[0].wait()
+    mine = table.at[core]
     each_peer(
-        over_z, lambda peer: push(over_z, expo_hbm, table.at[layers + (z - peer + NZ) % NZ - 1], sem_ez, peer)
+        over_z, lambda peer: push(over_z, mine, table.at[layers + (z - peer + NZ) % NZ - 1], sem_ez, peer)
     )
     for dy in (2, 1, 3, 0):
         for side in (1 - core, core)[: 1 if dy == 0 else 2]:
-            push(everyone, expo_hbm, table.at[2 * dy + core], sem_ej, device(0, NY - dy, side), 3 if dy == 2 else 1)
+            push(everyone, mine, table.at[2 * dy + core], sem_ej, device(0, NY - dy, side), 3 if dy == 2 else 1)
     for side in range(2):
-        push(everyone, expo_hbm, table.at[14 + core], sem_ej, device(NZ - 1, NY - 1, side))
+        push(everyone, mine, table.at[14 + core], sem_ej, device(NZ - 1, NY - 1, side))
 
     reads[1].wait()
     reads[5].wait()
@@ -213,7 +215,6 @@
 
     loop(chunks // 2, convert)
 
-    reads[0].wait()
     arrived(over_z, table.at[pl.ds(0, NZ - 1)], sem_ez)
 
     push(near, table.at[pl.ds(layers, 3)], table.at[pl.ds(layers, 3)], sem_ej, pair + 1 - core)
@@ -270,12 +271,12 @@
                 picked = sum3(jnp.dot(tparts[...], onehot, preferred_element_type=F32))
                 value = jnp.sum(jnp.where(lanes == lane_of[b, :, cols], picked, 0.0), axis=0, keepdims=True)
                 found = jnp.where(sublane == b, value, found)
-            mine = x * CW + c
+            own = x * CW + c
             if h == 0:
-                shuf[mine] = found
+                shuf[own] = found
             else:
-                shuf[mine] = shuf[mine] + found
-                each_peer(over_x, lambda peer: push(over_x, shuf.at[mine], shuf.at[mine], sem_sh, peer))
+                shuf[own] = shuf[own] + found
+                each_peer(over_x, lambda peer: push(over_x, shuf.at[own], shuf.at[own], sem_sh, peer))
 
         loop(CW, lookup)
 

time: 47.2 us -> 46.8 us (level)
  no operation moved by 1% of the time
where the time goes in v7:
time: 46.8 us; the launch traced here: 46.7 us
  Pallas kernels  46 us (98%)
  between operations  0.64 us (1%)
    pallas_call x1, Pallas kernels, local(): pl.pallas_call(functools.partial(kernel, dims), out_shape=outs, in_specs=...  45.4 us

profile of v7, /device:TPU:1, one launch (start us, length us, event | category | flops | bytes accessed | tf_op | source)
XLA Modules:
  0.0 46.7 jit_solution(13410589786279754633)
XLA Ops:
  0.6 45.4 %shard_map.129 = (f32[8,2048]{1,0:T(8,128)S(1)}, f32[8,2048]{1,0:T(8,128)S(1)}, f32[8,2048]{1,0:T(8,128)S(1)}, f32[16,512]{1,0:T(8,128)S(1)}) custom-call(s32[2048,2048]{1,0:T(8,128)} %geno_hbm.1, s32[2048,512]{1,0:T(8,128)} %tgeno_hbm.1, s32[1,2048]{1,0:T(1,128)} %bitcast.3, s32[1,512]{1,0:T(1,128)} %bitcast.5, f32[16,128]{1,0:T(8,128)} %bitcast.4, ...), custom_call_target="tpu_custom_call" | custom-call | tf_op jit(solution)/shard_map/pallas_call | solution.py:496
  46.0 0.7 %shard_map.130 = (f32[8,2048]{1,0:T(8,128)}, f32[8,2048]{1,0:T(8,128)}, f32[8,2048]{1,0:T(8,128)}, f32[16,512]{1,0:T(8,128)}) custom-call(f32[8,2048]{1,0:T(8,128)S(1)} %get-tuple-element.8.refs_0_, f32[8,2048]{1,0:T(8,128)S(1)} %get-tuple-element.9.refs_1_, f32[8,2048]{1,0:T(8,128)S(1)} %get-tuple-element.10.refs_2_, f32[16,512]{1,0:T(8,128)S(1)} %get-tuple-element.11.refs_3_), custom_call_target="tpu_custom_call" | custom-call | tf_op jit(solution)/shard_map/pallas_call | solution.py:575
